TPU v7x, 32 devices: a whole 2x2x4 slice. The times are simulated.
32 devices in a mesh: dp: 4 (over x, core), mp: 8 (over z, y).
Axes of the slice: x: 2, y: 2, z: 4, core: 2. Of those that a mesh axis runs over, the one named last changes fastest.
Arguments:
- tokens: bfloat16 [2048, 2048], P('dp', 'mp'), may hold values from -6 to 6
- cotangent: bfloat16 [2048, 2048], P('dp', 'mp'), may hold values from -6 to 6
- segment_ids: int32 [4, 512], P('dp'), may hold values from 0 to 5, never falling along the last dimension, each value on 1 to 256 neighbouring positions
- attention_gain: bfloat16 [2048], P('mp'), may hold values from 0.5 to 1.5
- feedforward_gain: bfloat16 [2048], P('mp'), may hold values from 0.5 to 1.5
- query_weight: bfloat16 [2048, 2048], P('mp'), may hold values from -0.125 to 0.125
- key_weight: bfloat16 [2048, 2048], P('mp'), may hold values from -0.125 to 0.125
- value_weight: bfloat16 [2048, 2048], P('mp'), may hold values from -0.125 to 0.125
- output_weight: bfloat16 [2048, 2048], P('mp'), may hold values from -0.125 to 0.125
- gate_weight: bfloat16 [2048, 5632], P('mp'), may hold values from -0.125 to 0.125
- up_weight: bfloat16 [2048, 5632], P('mp'), may hold values from -0.125 to 0.125
- down_weight: bfloat16 [5632, 2048], P('mp'), may hold values from -0.078125 to 0.078125
- query_left: float32 [2048, 16], P('mp'), may hold values from -0.125 to 0.125
- query_right: float32 [16, 2048], replicated, may hold values from -0.3 to 0.3
- query_magnitude: float32 [2048], replicated, may hold values from 1 to 2.5
- key_left: float32 [2048, 16], P('mp'), may hold values from -0.125 to 0.125
- key_right: float32 [16, 2048], replicated, may hold values from -0.3 to 0.3
- key_magnitude: float32 [2048], replicated, may hold values from 1 to 2.5
- value_left: float32 [2048, 16], P('mp'), may hold values from -0.125 to 0.125
- value_right: float32 [16, 2048], replicated, may hold values from -0.3 to 0.3
- value_magnitude: float32 [2048], replicated, may hold values from 0.5 to 1.5
- output_left: float32 [2048, 16], P('mp'), may hold values from -0.125 to 0.125
- output_right: float32 [16, 2048], replicated, may hold values from -0.3 to 0.3
- output_magnitude: float32 [2048], replicated, may hold values from 4 to 16
- gate_left: float32 [2048, 16], P('mp'), may hold values from -0.125 to 0.125
- gate_right: float32 [16, 5632], replicated, may hold values from -0.3 to 0.3
- gate_magnitude: float32 [5632], replicated, may hold values from 0.5 to 1.5
- up_left: float32 [2048, 16], P('mp'), may hold values from -0.125 to 0.125
- up_right: float32 [16, 5632], replicated, may hold values from -0.3 to 0.3
- up_magnitude: float32 [5632], replicated, may hold values from 0.5 to 1.5
- down_left: float32 [5632, 16], P('mp'), may hold values from -0.078125 to 0.078125
- down_right: float32 [16, 2048], replicated, may hold values from -0.3 to 0.3
- down_magnitude: float32 [2048], replicated, may hold values from 0.5 to 1.5
Outputs:
- layer_out: bfloat16 [2048, 2048], P('dp', 'mp')
- input_gradient: float32 [2048, 2048], P('dp', 'mp')
- query_left_gradient: float32 [2048, 16], P('mp')
- query_right_gradient: float32 [16, 2048], P(None, 'mp')
- query_magnitude_gradient: float32 [2048], P('mp')
- key_left_gradient: float32 [2048, 16], P('mp')
- key_right_gradient: float32 [16, 2048], P(None, 'mp')
- key_magnitude_gradient: float32 [2048], P('mp')
- value_left_gradient: float32 [2048, 16], P('mp')
- value_right_gradient: float32 [16, 2048], P(None, 'mp')
- value_magnitude_gradient: float32 [2048], P('mp')
- output_left_gradient: float32 [2048, 16], P('mp')
- output_right_gradient: float32 [16, 2048], P(None, 'mp')
- output_magnitude_gradient: float32 [2048], P('mp')
- gate_left_gradient: float32 [2048, 16], P('mp')
- gate_right_gradient: float32 [16, 5632], P(None, 'mp')
- gate_magnitude_gradient: float32 [5632], P('mp')
- up_left_gradient: float32 [2048, 16], P('mp')
- up_right_gradient: float32 [16, 5632], P(None, 'mp')
- up_magnitude_gradient: float32 [5632], P('mp')
- down_left_gradient: float32 [5632, 16], P('mp')
- down_right_gradient: float32 [16, 2048], P(None, 'mp')
- down_magnitude_gradient: float32 [2048], P('mp')
- statistics: float32 [7, 2], replicated
Inputs may be any that keep to these rules, and one draw needn't show every extreme that they name: `segment_ids`: segment numbers never fall along a row; each row holds 6 segments, none empty, none longer than 256 tokens.
All inputs are finite; a program needn't handle non-finite values.
Results may differ from a plain program's by a relative error of at most 0.012.
The roundings to bfloat16 on the way count: a program that leaves them out, or rounds other values in their place, can miss the bound.
Values may be sent and summed in bfloat16 or wider, within the bound.
No kernel may reach another device: no remote copies, remote signals or barrier semaphores. Data moves between devices by JAX's collectives and lax.ppermute only.
A program may use at most 256 MiB of HBM per device.

v0:
```python
import jax
import jax.numpy as jnp
from jax import lax
from jax.sharding import PartitionSpec as P

HD = 128
R = 16
ALPHA = 32


EPS = 1e-05
THETA = 10000.0
NEGATIVE = -1e30
HIGHEST = lax.Precision.HIGHEST


def contract_rows(left_part, right_part):
    return lax.dot_general(
        left_part, right_part, (((0,), (0,)), ((), ())), preferred_element_type=jnp.float32
    )


def precise_rows(left_part, right_part):
    return lax.dot_general(left_part, right_part, (((0,), (0,)), ((), ())), precision=HIGHEST)


def precise_cols(left_part, right_part):
    return lax.dot_general(left_part, right_part, (((1,), (1,)), ((), ())), precision=HIGHEST)


def row_total(values):
    return lax.psum(jnp.sum(values, axis=0), "mp")


def rank_total(values):
    return lax.psum(values, "mp")


def norm_forward(field, gain, model_width):
    inverse = lax.rsqrt(row_total(field * field) / model_width + EPS)
    return ((field * inverse[None, :] * gain[:, None]).astype(jnp.bfloat16), inverse)


def norm_backward(field, inverse, gain, grads, model_width):
    scaled = gain[:, None] * grads
    summed = row_total(scaled * field)
    return inverse[None, :] * scaled - field * (inverse**3 * summed / model_width)[None, :]


def gradient_adder(kept, shard_piece):
    return jnp.einsum("nrc,nct->rt", kept, shard_piece, preferred_element_type=jnp.float32)


def project_in(normed, stacked):
    members, rows_here, outputs_all = stacked.shape
    column_count = outputs_all // lax.axis_size("mp")
    tokens_here = normed.shape[1]

    def partial_term(offset, row_count):
        blocks = row_count // (members * column_count)
        pieces = jnp.einsum("nrc,rt->nct", stacked, normed, preferred_element_type=jnp.float32)
        pieces = pieces.reshape(members, blocks, column_count, tokens_here).transpose(1, 0, 2, 3)
        return pieces.reshape(row_count, tokens_here)

    own_rows = lax.psum_scatter(
        partial_term(jnp.int32(0), members * column_count * lax.axis_size("mp")),
        "mp",
        scatter_dimension=0,
        tiled=True,
    )
    return (own_rows.reshape(members, column_count, tokens_here), stacked)


def project_in_back(grads, kept):
    return gradient_adder(kept, lax.all_gather(grads, "mp", axis=1, tiled=True))


def project_output(values, weight):
    column_count = weight.shape[1] // lax.axis_size("mp")

    def partial_term(offset, row_count):
        return contract_rows(weight, values)

    return lax.psum_scatter(
        partial_term(jnp.int32(0), column_count * lax.axis_size("mp")),
        "mp",
        scatter_dimension=0,
        tiled=True,
    )


def project_down(values, weight):
    column_count = weight.shape[1] // lax.axis_size("mp")

    def partial_term(offset, row_count):
        return contract_rows(weight, values)

    return lax.psum_scatter(
        partial_term(jnp.int32(0), column_count * lax.axis_size("mp")),
        "mp",
        scatter_dimension=0,
        tiled=True,
    )


def project_middle_back(grads, weight):
    return jnp.dot(
        weight, lax.all_gather(grads, "mp", axis=0, tiled=True), preferred_element_type=jnp.float32
    )


def finish(base, right_own, rank_rows, factor, factor_scale):
    shaped = base + factor_scale * jnp.dot(right_own.T, rank_rows, precision=HIGHEST)
    return (shaped, shaped * factor[:, None])


def adapter_back(grads, shaped, factor, right_own, rank_rows, factor_scale):
    grad_low = (grads * factor[:, None]).astype(jnp.bfloat16)
    grad_full = grad_low.astype(jnp.float32)
    scale_grad = jnp.sum(grads * shaped, axis=1)
    right_term = factor_scale * precise_cols(rank_rows, grad_full)
    rank_part = jnp.dot(right_own, grad_full, precision=HIGHEST)
    return (grad_low, scale_grad, right_term, rank_part)


def masked_logits(query_block, key_rows, seg_block, segments, index_block, key_index, head_dim):
    raw_scores = lax.dot_general(
        query_block, key_rows, (((0,), (0,)), ((), ())), preferred_element_type=jnp.float32
    )
    allowed = (seg_block[:, None] == segments[None, :]) & (
        key_index[None, :] <= index_block[:, None]
    )
    return jnp.where(allowed, raw_scores * head_dim ** (-0.5), NEGATIVE)


def attention_forward(queries, key_set, value_set, segment_set, block):
    pair_count, head_dim, length = queries.shape
    block_count = length // block
    key_index = jnp.arange(length, dtype=jnp.int32)

    def one_pair(items):
        query_rows, key_rows, value_rows, segments = items

        def one_block(parts_in):
            query_block, seg_block, index_block = parts_in
            logits = masked_logits(
                query_block, key_rows, seg_block, segments, index_block, key_index, head_dim
            )
            highest = jnp.max(logits, axis=1, keepdims=True)
            powers = jnp.exp(logits - highest)
            totals = jnp.sum(powers, axis=1, keepdims=True)
            weights_low = (powers / totals).astype(jnp.bfloat16)
            block_out = lax.dot_general(
                value_rows,
                weights_low,
                (((1,), (1,)), ((), ())),
                preferred_element_type=jnp.float32,
            )
            return (block_out, (highest + jnp.log(totals))[:, 0])

        blocks_in = (
            query_rows.reshape(head_dim, block_count, block).transpose(1, 0, 2),
            segments.reshape(block_count, block),
            key_index.reshape(block_count, block),
        )
        blocks_out, log_totals = lax.map(one_block, blocks_in)
        return (blocks_out.transpose(1, 0, 2).reshape(head_dim, length), log_totals.reshape(length))

    return lax.map(one_pair, (queries, key_set, value_set, segment_set))


def attention_backward(queries, key_set, value_set, segment_set, grad_set, total_set, block):
    pair_count, head_dim, length = queries.shape
    block_count = length // block
    key_index = jnp.arange(length, dtype=jnp.int32)

    def one_pair(items):
        query_rows, key_rows, value_rows, segments, grad_rows, total_rows = items

        def one_block(carry, parts_in):
            key_grad, value_grad = carry
            query_block, grad_block, total_block, seg_block, index_block = parts_in
            logits = masked_logits(
                query_block, key_rows, seg_block, segments, index_block, key_index, head_dim
            )
            probs = jnp.exp(logits - total_block[:, None])
            probs_low = probs.astype(jnp.bfloat16)
            prob_grad = lax.dot_general(
                grad_block, value_rows, (((0,), (0,)), ((), ())), preferred_element_type=jnp.float32
            )
            deltas = jnp.sum(prob_grad * probs, axis=1, keepdims=True)
            score_grad = (probs * (prob_grad - deltas) * head_dim ** (-0.5)).astype(jnp.bfloat16)
            query_grad = lax.dot_general(
                key_rows, score_grad, (((1,), (1,)), ((), ())), preferred_element_type=jnp.float32
            )
            key_grad = key_grad + lax.dot_general(
                query_block,
                score_grad,
                (((1,), (0,)), ((), ())),
                preferred_element_type=jnp.float32,
            )
            value_grad = value_grad + lax.dot_general(
                grad_block, probs_low, (((1,), (0,)), ((), ())), preferred_element_type=jnp.float32
            )
            return ((key_grad, value_grad), query_grad)

        blocks_in = (
            query_rows.reshape(head_dim, block_count, block).transpose(1, 0, 2),
            grad_rows.reshape(head_dim, block_count, block).transpose(1, 0, 2),
            total_rows.reshape(block_count, block),
            segments.reshape(block_count, block),
            key_index.reshape(block_count, block),
        )
        zero_grad = jnp.zeros((head_dim, length), jnp.float32)
        (key_grad, value_grad), query_blocks = lax.scan(
            one_block, (zero_grad, zero_grad), blocks_in
        )
        return (query_blocks.transpose(1, 0, 2).reshape(head_dim, length), key_grad, value_grad)

    return lax.map(one_pair, (queries, key_set, value_set, segment_set, grad_set, total_set))


def on_device(
    tokens,
    cotangent,
    segment_ids,
    attention_gain,
    feedforward_gain,
    query_weight,
    key_weight,
    value_weight,
    output_weight,
    gate_weight,
    up_weight,
    down_weight,
    query_left,
    query_right,
    query_magnitude,
    key_left,
    key_right,
    key_magnitude,
    value_left,
    value_right,
    value_magnitude,
    output_left,
    output_right,
    output_magnitude,
    gate_left,
    gate_right,
    gate_magnitude,
    up_left,
    up_right,
    up_magnitude,
    down_left,
    down_right,
    down_magnitude,
):
    factor_scale = ALPHA / R
    devices_mp = lax.axis_size("mp")
    device_place = lax.axis_index("mp")
    weights = (
        query_weight,
        key_weight,
        value_weight,
        output_weight,
        gate_weight,
        up_weight,
        down_weight,
    )
    lefts = (query_left, key_left, value_left, output_left, gate_left, up_left, down_left)
    rights = (query_right, key_right, value_right, output_right, gate_right, up_right, down_right)
    magnitudes = (
        query_magnitude,
        key_magnitude,
        value_magnitude,
        output_magnitude,
        gate_magnitude,
        up_magnitude,
        down_magnitude,
    )
    fulls = [
        weight.astype(jnp.float32)
        + factor_scale * jnp.dot(left_factor, right_factor, precision=HIGHEST)
        for weight, left_factor, right_factor in zip(weights, lefts, rights)
    ]
    squares = [jnp.sum(adapted_full * adapted_full, axis=0) for adapted_full in fulls]
    squares = lax.psum(
        (squares[0], squares[1], squares[2], squares[3], squares[4], squares[5], squares[6]), "mp"
    )
    norms = [jnp.sqrt(square_sum) for square_sum in squares]
    crossed = [
        precise_rows(left_factor, adapted_full) for left_factor, adapted_full in zip(lefts, fulls)
    ]
    crossed = (
        lax.psum_scatter(
            crossed[0].astype(jnp.bfloat16), "mp", scatter_dimension=1, tiled=True
        ).astype(jnp.float32),
        lax.psum_scatter(
            crossed[1].astype(jnp.bfloat16), "mp", scatter_dimension=1, tiled=True
        ).astype(jnp.float32),
        lax.psum_scatter(
            crossed[2].astype(jnp.bfloat16), "mp", scatter_dimension=1, tiled=True
        ).astype(jnp.float32),
        lax.psum_scatter(
            crossed[3].astype(jnp.bfloat16), "mp", scatter_dimension=1, tiled=True
        ).astype(jnp.float32),
        lax.psum_scatter(
            crossed[4].astype(jnp.bfloat16), "mp", scatter_dimension=1, tiled=True
        ).astype(jnp.float32),
        lax.psum_scatter(
            crossed[5].astype(jnp.bfloat16), "mp", scatter_dimension=1, tiled=True
        ).astype(jnp.float32),
        lax.psum_scatter(
            crossed[6].astype(jnp.bfloat16), "mp", scatter_dimension=1, tiled=True
        ).astype(jnp.float32),
    )
    column_counts = [weight.shape[1] // devices_mp for weight in weights]
    own_norms = [
        lax.dynamic_slice_in_dim(column_norm, device_place * column_count, column_count)
        for column_norm, column_count in zip(norms, column_counts)
    ]
    own_magnitudes = [
        lax.dynamic_slice_in_dim(magnitude, device_place * column_count, column_count)
        for magnitude, column_count in zip(magnitudes, column_counts)
    ]
    own_rights = [
        lax.dynamic_slice_in_dim(right_factor, device_place * column_count, column_count, 1)
        for right_factor, column_count in zip(rights, column_counts)
    ]
    factors = [magnitude / column_norm for magnitude, column_norm in zip(own_magnitudes, own_norms)]
    tokens_field = tokens.T.astype(jnp.float32)
    rows_local, seq_length = segment_ids.shape
    features_here = tokens_field.shape[0]
    model_width = features_here * devices_mp
    rank_size = query_left.shape[1]
    head_dim = HD
    heads_here = features_here // head_dim
    gain_first = attention_gain.astype(jnp.float32)
    gain_second = feedforward_gain.astype(jnp.float32)
    attention_stack = jnp.stack((query_weight, key_weight, value_weight))
    feed_stack = jnp.stack((gate_weight, up_weight))
    shaped = [None] * 7
    outputs = [None] * 7
    rank_rows = [None] * 7

    def rank_rows_of(members, normed_full):
        pieces = [jnp.dot(lefts[member].T, normed_full, precision=HIGHEST) for member in members]
        summed = rank_total(jnp.concatenate(pieces, axis=0))
        for slot, member in enumerate(members):
            rank_rows[member] = summed[slot * rank_size : (slot + 1) * rank_size]

    normed_one, inverse_one = norm_forward(tokens_field, gain_first, model_width)
    normed_one_full = normed_one.astype(jnp.float32)
    rank_rows_of((0, 1, 2), normed_one_full)
    bases_one, kept_one = project_in(normed_one, attention_stack)
    for member in range(3):
        shaped[member], outputs[member] = finish(
            bases_one[member], own_rights[member], rank_rows[member], factors[member], factor_scale
        )
    key_index = jnp.arange(seq_length, dtype=jnp.int32)
    change = jnp.concatenate(
        [
            jnp.ones((rows_local, 1), jnp.int32),
            (segment_ids[:, 1:] != segment_ids[:, :-1]).astype(jnp.int32),
        ],
        axis=1,
    )
    begins = lax.cummax(key_index[None, :] * change, axis=1)
    places = (key_index[None, :] - begins).astype(jnp.float32)
    half_dim = head_dim // 2
    freqs = THETA ** (-2.0 * jnp.arange(half_dim, dtype=jnp.float32) / head_dim)
    angles = freqs[:, None, None] * places[None]
    cosine = jnp.cos(angles)
    sine = jnp.sin(angles)

    def split_heads(values):
        return values.reshape(heads_here, head_dim, rows_local, seq_length)

    def merge_heads(values):
        return values.reshape(heads_here * head_dim, rows_local * seq_length)

    def rotate(values, turning):
        first_half = values[:, :half_dim]
        second_half = values[:, half_dim:]
        return jnp.concatenate(
            [
                first_half * cosine - turning * second_half * sine,
                second_half * cosine + turning * first_half * sine,
            ],
            axis=1,
        )

    def to_pairs(values):
        return values.transpose(0, 2, 1, 3).reshape(heads_here * rows_local, head_dim, seq_length)

    def from_pairs(values):
        return values.reshape(heads_here, rows_local, head_dim, seq_length).transpose(0, 2, 1, 3)

    query_pairs = to_pairs(rotate(split_heads(outputs[0]), 1.0)).astype(jnp.bfloat16)
    key_pairs = to_pairs(rotate(split_heads(outputs[1]), 1.0)).astype(jnp.bfloat16)
    value_pairs = to_pairs(split_heads(outputs[2])).astype(jnp.bfloat16)
    segment_pairs = jnp.tile(segment_ids, (heads_here, 1))
    block = min(512, seq_length)
    attended, log_totals = attention_forward(
        query_pairs, key_pairs, value_pairs, segment_pairs, block
    )
    mixed = merge_heads(from_pairs(attended)).astype(jnp.bfloat16)
    mixed_full = mixed.astype(jnp.float32)
    rank_rows_of((3,), mixed_full)
    base_out = project_output(mixed, output_weight)
    shaped[3], outputs[3] = finish(base_out, own_rights[3], rank_rows[3], factors[3], factor_scale)
    middle = tokens_field + outputs[3]
    normed_two, inverse_two = norm_forward(middle, gain_second, model_width)
    normed_two_full = normed_two.astype(jnp.float32)
    rank_rows_of((4, 5), normed_two_full)
    bases_two, kept_two = project_in(normed_two, feed_stack)
    for member in (4, 5):
        shaped[member], outputs[member] = finish(
            bases_two[member - 4],
            own_rights[member],
            rank_rows[member],
            factors[member],
            factor_scale,
        )
    gate = outputs[4]
    upper = outputs[5]
    sigma = jax.nn.sigmoid(gate)
    activated = (gate * sigma * upper).astype(jnp.bfloat16)
    activated_full = activated.astype(jnp.float32)
    rank_rows_of((6,), activated_full)
    base_down = project_down(activated, down_weight)
    shaped[6], outputs[6] = finish(base_down, own_rights[6], rank_rows[6], factors[6], factor_scale)
    result = middle + outputs[6]
    layer_out = result.T.astype(jnp.bfloat16)
    left_terms = [None] * 7
    right_terms = [None] * 7
    scale_terms = [None] * 7

    def settle(member):
        left_terms[member], right_terms[member], scale_terms[member] = lax.psum(
            (left_terms[member], right_terms[member], scale_terms[member]), "dp"
        )

    def backward_group(members, grads_out, normed_full):
        lowered = []
        partials = []
        for slot, member in enumerate(members):
            grad_low, scale_terms[member], right_terms[member], rank_part = adapter_back(
                grads_out[slot],
                shaped[member],
                factors[member],
                own_rights[member],
                rank_rows[member],
                factor_scale,
            )
            lowered.append(grad_low)
            partials.append(rank_part)
        rank_grads = rank_total(jnp.concatenate(partials, axis=0))
        extra = jnp.zeros_like(normed_full)
        for slot, member in enumerate(members):
            rank_grad = rank_grads[slot * rank_size : (slot + 1) * rank_size]
            left_terms[member] = factor_scale * precise_cols(normed_full, rank_grad)
            extra = extra + factor_scale * jnp.dot(lefts[member], rank_grad, precision=HIGHEST)
            settle(member)
        return (lowered, extra)

    incoming = cotangent.T.astype(jnp.float32)
    lowered, extra = backward_group((6,), (incoming,), activated_full)
    grad_activated = project_middle_back(lowered[0], down_weight) + extra
    silu_gate = gate * sigma
    grad_gate = grad_activated * upper * (sigma * (1.0 + gate * (1.0 - sigma)))
    grad_upper = grad_activated * silu_gate
    lowered, extra = backward_group((4, 5), (grad_gate, grad_upper), normed_two_full)
    grad_normed_two = project_in_back(jnp.stack(lowered), kept_two) + extra
    grad_middle = incoming + norm_backward(
        middle, inverse_two, gain_second, grad_normed_two, model_width
    )
    lowered, extra = backward_group((3,), (grad_middle,), mixed_full)
    grad_mixed = (project_middle_back(lowered[0], output_weight) + extra).astype(jnp.bfloat16)
    grad_pairs = to_pairs(split_heads(grad_mixed))
    query_grads, key_grads, value_grads = attention_backward(
        query_pairs, key_pairs, value_pairs, segment_pairs, grad_pairs, log_totals, block
    )
    grad_query = merge_heads(rotate(from_pairs(query_grads), -1.0))
    grad_key = merge_heads(rotate(from_pairs(key_grads), -1.0))
    grad_value = merge_heads(from_pairs(value_grads))
    lowered, extra = backward_group((0, 1, 2), (grad_query, grad_key, grad_value), normed_one_full)
    grad_normed_one = project_in_back(jnp.stack(lowered), kept_one) + extra
    grad_tokens = grad_middle + norm_backward(
        tokens_field, inverse_one, gain_first, grad_normed_one, model_width
    )
    input_gradient = grad_tokens.T
    magnitude_grads = [scale_terms[member] / own_norms[member] for member in range(7)]
    own_ratios = [
        -scale_terms[member] * own_magnitudes[member] / own_norms[member] ** 3
        for member in range(7)
    ]
    full_ratios = (
        lax.all_gather(own_ratios[0], "mp", axis=0, tiled=True),
        lax.all_gather(own_ratios[1], "mp", axis=0, tiled=True),
        lax.all_gather(own_ratios[2], "mp", axis=0, tiled=True),
        lax.all_gather(own_ratios[3], "mp", axis=0, tiled=True),
        lax.all_gather(own_ratios[4], "mp", axis=0, tiled=True),
        lax.all_gather(own_ratios[5], "mp", axis=0, tiled=True),
        lax.all_gather(own_ratios[6], "mp", axis=0, tiled=True),
    )
    left_grads = [
        left_terms[member]
        + factor_scale * precise_cols(fulls[member] * full_ratios[member][None, :], rights[member])
        for member in range(7)
    ]
    right_grads = [
        right_terms[member] + factor_scale * own_ratios[member][None, :] * crossed[member]
        for member in range(7)
    ]
    stat_rows = [
        jnp.stack(
            [jnp.sqrt(jnp.mean((magnitudes[member] - norms[member]) ** 2)), jnp.mean(norms[member])]
        )
        for member in range(7)
    ]
    statistics = jnp.stack(stat_rows)
    return (
        layer_out,
        input_gradient,
        left_grads[0],
        right_grads[0],
        magnitude_grads[0],
        left_grads[1],
        right_grads[1],
        magnitude_grads[1],
        left_grads[2],
        right_grads[2],
        magnitude_grads[2],
        left_grads[3],
        right_grads[3],
        magnitude_grads[3],
        left_grads[4],
        right_grads[4],
        magnitude_grads[4],
        left_grads[5],
        right_grads[5],
        magnitude_grads[5],
        left_grads[6],
        right_grads[6],
        magnitude_grads[6],
        statistics,
    )


def solution(mesh):
    placed = (
        P("dp", "mp"),
        P("dp", "mp"),
        P("dp", None),
        P("mp"),
        P("mp"),
        P("mp", None),
        P("mp", None),
        P("mp", None),
        P("mp", None),
        P("mp", None),
        P("mp", None),
        P("mp", None),
        P("mp", None),
        P(),
        P(),
        P("mp", None),
        P(),
        P(),
        P("mp", None),
        P(),
        P(),
        P("mp", None),
        P(),
        P(),
        P("mp", None),
        P(),
        P(),
        P("mp", None),
        P(),
        P(),
        P("mp", None),
        P(),
        P(),
    )
    return jax.shard_map(
        on_device,
        mesh=mesh,
        in_specs=placed,
        out_specs=(
            P("dp", "mp"),
            P("dp", "mp"),
            P("mp", None),
            P(None, "mp"),
            P("mp"),
            P("mp", None),
            P(None, "mp"),
            P("mp"),
            P("mp", None),
            P(None, "mp"),
            P("mp"),
            P("mp", None),
            P(None, "mp"),
            P("mp"),
            P("mp", None),
            P(None, "mp"),
            P("mp"),
            P("mp", None),
            P(None, "mp"),
            P("mp"),
            P("mp", None),
            P(None, "mp"),
            P("mp"),
            P(),
        ),
        check_vma=False,
    )
```

profile of v0, /device:TPU:0, one launch (start us, length us, event | category | flops | bytes accessed | tf_op | source)
XLA Modules:
  0.0 2182.1 jit_solution(12133969497117053770)
XLA Ops:
  19.1 38.9 %all-reduce.5 = (f32[512]{0:T(512)S(1)}, f32[2048]{0:T(1024)S(1)}, f32[2048]{0:T(1024)S(1)}, f32[2048]{0:T(1024)S(1)}) all-reduce(f32[512]{0:T(512)S(1)} %fusion.156, f32[2048]{0:T(1024)S(1)} %get-tuple-element.458, f32[2048]{0:T(1024)S(1)} %get-tuple-element.460, f32[2048]{0:T(1024)S(1)} %get-tuple-element.462), channel_id=1, replica_groups=mesh['dp'=4,'mp'=8] {'mp'}, use_global_device_ids=true, to_apply=%region_1.0 | all-reduce | flops 6656 | bytes 53248 | tf_op jit(solution)/shard_map/psum | solution.py:32
  74.7 11.5 copy.97
  101.9 25.3 %all-reduce.16.cloned.1.call-done = f32[48,512]{1,0:T(8,128)} async-done(((f32[48,512]{1,0:T(8,128)}), f32[48,512]{1,0:T(8,128)}) %all-reduce.16.cloned.1.call-update) | async-done | bytes 98320 | tf_op jit(solution)/shard_map/psum | solution.py:36
  127.1 210.1 %reduce-scatter.16.cloned.1.call-done = f32[768,512]{1,0:T(8,128)} async-done(((f32[6144,512]{1,0:T(8,128)}), f32[768,512]{1,0:T(8,128)}) %reduce-scatter.16.cloned.1.call-update) | async-done | bytes 1572880 | tf_op jit(solution)/shard_map/reduce_scatter | solution.py:65
  387.7 37.1 %all-reduce.4 = (f32[16,512]{1,0:T(8,128)}, f32[2048]{0:T(1024)S(1)}, f32[2048]{0:T(1024)S(1)}) all-reduce(f32[16,512]{1,0:T(8,128)S(1)} %convolution_bitcast_fusion.9, f32[2048]{0:T(1024)S(1)} %copy-done.83, f32[2048]{0:T(1024)S(1)} %get-tuple-element.472), channel_id=1, replica_groups=mesh['dp'=4,'mp'=8] {'mp'}, use_global_device_ids=true, to_apply=%region_17.0 | all-reduce | flops 12288 | bytes 98304 | tf_op jit(solution)/shard_map/psum | solution.py:36
  429.3 17.4 reduce-scatter.18.cloned.1.call-done
  460.3 61.1 %all-reduce.26.cloned.1.call-done = (f32[512]{0:T(512)}, f32[5632]{0:T(1024)}, f32[5632]{0:T(1024)}, f32[16,512]{1,0:T(8,128)}) async-done(((f32[512]{0:T(512)}, f32[5632]{0:T(1024)}, f32[5632]{0:T(1024)}, f32[16,512]{1,0:T(8,128)}), (f32[512]{0:T(512)}, f32[5632]{0:T(1024)}, f32[5632]{0:T(1024)}, f32[16,512]{1,0:T(8,128)})) %all-reduce.26.cloned.1.call-update) | async-done | bytes 79888 | tf_op jit(solution)/shard_map/psum | solution.py:32
  525.8 13.5 fusion.55
  539.3 16.3 copy.101
  555.7 16.6 all-gather.10.cloned.1.call-done
  581.8 61.7 %all-reduce.18.cloned.1.call-done = f32[32,512]{1,0:T(8,128)} async-done(((f32[32,512]{1,0:T(8,128)}), f32[32,512]{1,0:T(8,128)}) %all-reduce.18.cloned.1.call-update) | async-done | bytes 65552 | tf_op jit(solution)/shard_map/psum | solution.py:36
  643.4 376.7 %reduce-scatter.20.cloned.1.call-done = f32[1408,512]{1,0:T(8,128)} async-done(((f32[11264,512]{1,0:T(8,128)}), f32[1408,512]{1,0:T(8,128)}) %reduce-scatter.20.cloned.1.call-update) | async-done | bytes 2883600 | tf_op jit(solution)/shard_map/reduce_scatter | solution.py:65
  1035.4 65.7 %all-reduce.20.cloned.1.call-done = f32[32,512]{1,0:T(8,128)} async-done(((f32[32,512]{1,0:T(8,128)}), f32[32,512]{1,0:T(8,128)}) %all-reduce.20.cloned.1.call-update) | async-done | bytes 65552 | tf_op jit(solution)/shard_map/psum | solution.py:36
  1103.3 163.2 %all-gather.12.cloned.1.call-done = bf16[2,5632,512]{2,1,0:T(8,128)(2,1)} async-done(((bf16[2,704,512]{2,1,0:T(8,128)(2,1)}), bf16[2,5632,512]{2,1,0:T(8,128)(2,1)}) %all-gather.12.cloned.1.call-update) | async-done | bytes 11534352 | tf_op jit(solution)/shard_map/all_gather | solution.py:75
  1277.4 19.2 psum.295
  1302.9 35.5 %psum.296 = f32[16,512]{1,0:T(8,128)} all-reduce(f32[16,512]{1,0:T(8,128)} %fusion.197), channel_id=1, replica_groups=mesh['dp'=4,'mp'=8] {'mp'}, use_global_device_ids=true, to_apply=%region_36.37 | all-reduce | flops 8192 | bytes 65536 | tf_op jit(solution)/shard_map/psum | solution.py:36
  1351.3 12.9 while.31
  1395.0 48.2 %all-reduce.22.cloned.1.call-done = f32[48,512]{1,0:T(8,128)} async-done(((f32[48,512]{1,0:T(8,128)}), f32[48,512]{1,0:T(8,128)}) %all-reduce.22.cloned.1.call-update) | async-done | bytes 98320 | tf_op jit(solution)/shard_map/psum | solution.py:36
  1446.8 96.3 %all-gather.16.cloned.1.call-done = bf16[3,2048,512]{2,1,0:T(8,128)(2,1)} async-done(((bf16[3,256,512]{2,1,0:T(8,128)(2,1)}), bf16[3,2048,512]{2,1,0:T(8,128)(2,1)}) %all-gather.16.cloned.1.call-update) | async-done | bytes 6291472 | tf_op jit(solution)/shard_map/all_gather | solution.py:75
  1592.3 27.8 %all-reduce.24.cloned.1.call-done = (f32[16,512]{1,0:T(8,128)}, f32[512]{0:T(512)}, f32[5632]{0:T(1024)}, f32[5632]{0:T(1024)}) async-done(((f32[16,512]{1,0:T(8,128)}, f32[512]{0:T(512)}, f32[5632]{0:T(1024)}, f32[5632]{0:T(1024)}), (f32[16,512]{1,0:T(8,128)}, f32[512]{0:T(512)}, f32[5632]{0:T(1024)}, f32[5632]{0:T(1024)})) %all-reduce.24.cloned.1.call-update) | async-done | bytes 79888 | tf_op jit(solution)/shard_map/psum | solution.py:36
  1622.0 89.8 %reduce-scatter.22.cloned.1.call-done = f32[256,512]{1,0:T(8,128)} async-done(((f32[2048,512]{1,0:T(8,128)}), f32[256,512]{1,0:T(8,128)}) %reduce-scatter.22.cloned.1.call-update) | async-done | bytes 524304 | tf_op jit(solution)/shard_map/reduce_scatter | solution.py:98
  1738.7 41.6 %reduce-scatter.36.cloned.1.call-done = bf16[704,16]{1,0:T(8,128)(2,1)} async-done(((bf16[5632,16]{1,0:T(8,128)(2,1)}), bf16[704,16]{1,0:T(8,128)(2,1)}) %reduce-scatter.36.cloned.1.call-update) | async-done | bytes 22544
  1781.4 66.8 %reduce-scatter.34.cloned.1.call-done = bf16[704,16]{1,0:T(8,128)(2,1)} async-done(((bf16[5632,16]{1,0:T(8,128)(2,1)}), bf16[704,16]{1,0:T(8,128)(2,1)}) %reduce-scatter.34.cloned.1.call-update) | async-done | bytes 22544
  1859.3 27.1 %all-reduce.28.cloned.1.call-done = (f32[256,16]{0,1:T(8,128)}, f32[256]{0:T(256)}, f32[16,256]{1,0:T(8,128)}, f32[256,16]{0,1:T(8,128)}, f32[256]{0:T(256)}, /*...) async-done(((f32[256,16]{0,1:T(8,128)}, f32[256]{0:T(256)}, ...) | async-done | bytes 320528 | tf_op jit(solution)/shard_map/psum | solution.py:440
  1887.8 20.7 all-gather.4
  1909.8 16.3 all-gather.3
  1927.4 18.3 all-gather.2
  1947.1 16.3 all-gather.1
  1964.7 18.3 all-gather
  2017.7 42.1 %reduce-scatter.28.cloned.1.call-done = bf16[16,256]{1,0:T(8,128)(2,1)} async-done(((bf16[16,2048]{1,0:T(8,128)(2,1)}), bf16[16,256]{1,0:T(8,128)(2,1)}) %reduce-scatter.28.cloned.1.call-update) | async-done | bytes 8208 | tf_op jit(solution)/shard_map/reduce_scatter | solution.py:301
  2061.0 55.7 %reduce-scatter.26.cloned.1.call-done = bf16[16,256]{1,0:T(8,128)(2,1)} async-done(((bf16[16,2048]{1,0:T(8,128)(2,1)}), bf16[16,256]{1,0:T(8,128)(2,1)}) %reduce-scatter.26.cloned.1.call-update) | async-done | bytes 8208 | tf_op jit(solution)/shard_map/reduce_scatter | solution.py:298
  2118.1 55.7 %reduce-scatter.24.cloned.1.call-done = bf16[16,256]{1,0:T(8,128)(2,1)} async-done(((bf16[16,2048]{1,0:T(8,128)(2,1)}), bf16[16,256]{1,0:T(8,128)(2,1)}) %reduce-scatter.24.cloned.1.call-update) | async-done | bytes 8208 | tf_op jit(solution)/shard_map/reduce_scatter | solution.py:295
  (547 shorter events, 352.4 us)
Async XLA Ops:
  7.2 364.7 %copy-start = (f32[16,5632]{1,0:T(8,128)S(1)}, f32[16,5632]{1,0:T(8,128)}, u32[]{:S(2)}) copy-start(f32[16,5632]{1,0:T(8,128)} %param.65) | copy-start | bytes 1081348
  7.2 119.9 %all-reduce.16.cloned.1.call-start = ((), (), s32[]{:S(2)}) async-start(), calls=%async_computation.12 | async-start | bytes 196608 | tf_op jit(solution)/shard_map/psum | solution.py:36
  15.6 1716.9 %copy-start.1 = (f32[256,2048]{1,0:T(8,128)}, f32[256,2048]{1,0:T(8,128)S(1)}, u32[]{:S(2)}) copy-start(f32[256,2048]{1,0:T(8,128)S(1)} %get-tuple-element.461) | copy-start | bytes 6291460
  59.5 277.7 %reduce-scatter.16.cloned.1.call-start = ((), (), s32[]{:S(2)}) async-start(), calls=%async_computation.11 | async-start | bytes 14155776 | tf_op jit(solution)/shard_map/reduce_scatter | solution.py:65
  86.2 360.5 %reduce-scatter.18.cloned.1.call-start = ((), (), s32[]{:S(2)}) async-start(), calls=%async_computation.13 | async-start | bytes 4718592 | tf_op jit(solution)/shard_map/reduce_scatter | solution.py:84
  99.0 243.4 %copy-start.109 = (f32[256]{0:T(256)}, f32[256]{0:T(256)S(1)}, u32[]{:S(2)}) copy-start(f32[256]{0:T(256)S(1)} %dynamic-slice_divide_fusion.6) | copy-start | bytes 3076
  99.7 242.5 %copy-start.111 = (f32[256]{0:T(256)}, f32[256]{0:T(256)S(1)}, u32[]{:S(2)}) copy-start(f32[256]{0:T(256)S(1)} %dynamic-slice_divide_fusion.7) | copy-start | bytes 3076
  99.8 244.1 %copy-start.107 = (f32[256]{0:T(256)}, f32[256]{0:T(256)S(1)}, u32[]{:S(2)}) copy-start(f32[256]{0:T(256)S(1)} %dynamic-slice_divide_fusion.8) | copy-start | bytes 3076
  101.9 240.6 %copy-start.40 = (f32[64,512]{1,0:T(8,128)}, f32[64,512]{1,0:T(8,128)S(1)}, u32[]{:S(2)}) copy-start(f32[64,512]{1,0:T(8,128)S(1)} %get-tuple-element.457) | copy-start | bytes 393220
  357.6 163.7 %all-reduce.26.cloned.1.call-start = ((), (), s32[]{:S(2)}) async-start(), calls=%async_computation.31 | async-start | bytes 167936 | tf_op jit(solution)/shard_map/psum | solution.py:32
  449.9 122.5 %all-gather.10.cloned.1.call-start = ((), (), s32[]{:S(2)}) async-start(), calls=%async_computation.17 | async-start | bytes 2359296 | tf_op jit(solution)/shard_map/all_gather | solution.py:108
  450.5 192.9 %all-reduce.18.cloned.1.call-start = ((), (), s32[]{:S(2)}) async-start(), calls=%async_computation.15 | async-start | bytes 131072 | tf_op jit(solution)/shard_map/psum | solution.py:36
  525.3 494.9 %reduce-scatter.20.cloned.1.call-start = ((), (), s32[]{:S(2)}) async-start(), calls=%async_computation.14 | async-start | bytes 25952256 | tf_op jit(solution)/shard_map/reduce_scatter | solution.py:65
  555.7 545.4 %all-reduce.20.cloned.1.call-start = ((), (), s32[]{:S(2)}) async-start(), calls=%async_computation.19 | async-start | bytes 131072 | tf_op jit(solution)/shard_map/psum | solution.py:36
  1032.4 234.1 %all-gather.12.cloned.1.call-start = ((), (), s32[]{:S(2)}) async-start(), calls=%async_computation.18 | async-start | bytes 12976128 | tf_op jit(solution)/shard_map/all_gather | solution.py:75
  1035.1 312.8 %all-gather.14.cloned.1.call-start = ((), (), s32[]{:S(2)}) async-start(), calls=%async_computation.20 | async-start | bytes 2359296 | tf_op jit(solution)/shard_map/all_gather | solution.py:108
  1301.0 142.2 %all-reduce.22.cloned.1.call-start = ((), (), s32[]{:S(2)}) async-start(), calls=%async_computation.22 | async-start | bytes 196608 | tf_op jit(solution)/shard_map/psum | solution.py:36
  1374.4 168.7 %all-gather.16.cloned.1.call-start = ((), (), s32[]{:S(2)}) async-start(), calls=%async_computation.21 | async-start | bytes 7077888 | tf_op jit(solution)/shard_map/all_gather | solution.py:75
  1377.6 242.5 %all-reduce.24.cloned.1.call-start = ((), (), s32[]{:S(2)}) async-start(), calls=%async_computation.30 | async-start | bytes 167936 | tf_op jit(solution)/shard_map/psum | solution.py:36
  1551.6 160.3 %reduce-scatter.22.cloned.1.call-start = ((), (), s32[]{:S(2)}) async-start(), calls=%async_computation.16 | async-start | bytes 4718592 | tf_op jit(solution)/shard_map/reduce_scatter | solution.py:98
  1557.7 222.6 %reduce-scatter.36.cloned.1.call-start = ((), (), s32[]{:S(2)}) async-start(), calls=%async_computation.29 | async-start | bytes 1622016
  1566.5 281.7 %reduce-scatter.34.cloned.1.call-start = ((), (), s32[]{:S(2)}) async-start(), calls=%async_computation.28 | async-start | bytes 1622016
  1575.2 311.2 %all-reduce.28.cloned.1.call-start = ((), (), s32[]{:S(2)}) async-start(), calls=%async_computation.32 | async-start | bytes 665600 | tf_op jit(solution)/shard_map/psum | solution.py:440
  1715.0 300.0 %reduce-scatter.32.cloned.1.call-start = ((), (), s32[]{:S(2)}) async-start(), calls=%async_computation.27 | async-start | bytes 73728 | tf_op jit(solution)/shard_map/reduce_scatter | solution.py:313
  1721.9 294.5 %reduce-scatter.30.cloned.1.call-start = ((), (), s32[]{:S(2)}) async-start(), calls=%async_computation.26 | async-start | bytes 73728 | tf_op jit(solution)/shard_map/reduce_scatter | solution.py:304
  1725.4 334.3 %reduce-scatter.28.cloned.1.call-start = ((), (), s32[]{:S(2)}) async-start(), calls=%async_computation.25 | async-start | bytes 73728 | tf_op jit(solution)/shard_map/reduce_scatter | solution.py:301
  1728.9 387.9 %reduce-scatter.26.cloned.1.call-start = ((), (), s32[]{:S(2)}) async-start(), calls=%async_computation.24 | async-start | bytes 73728 | tf_op jit(solution)/shard_map/reduce_scatter | solution.py:298
  1728.9 127.2 %copy-start.126 = (f32[512]{0:T(512)S(1)}, f32[512]{0:T(512)}, u32[]{:S(2)}) copy-start(f32[512]{0:T(512)} %copy-done.125) | copy-start | bytes 6148
  1732.4 441.4 %reduce-scatter.24.cloned.1.call-start = ((), (), s32[]{:S(2)}) async-start(), calls=%async_computation.23 | async-start | bytes 73728 | tf_op jit(solution)/shard_map/reduce_scatter | solution.py:295
  1734.3 248.7 %copy-start.44 = (f32[16,2048]{1,0:T(8,128)S(1)}, f32[16,2048]{1,0:T(8,128)}, u32[]{:S(2)}) copy-start(f32[16,2048]{1,0:T(8,128)} %param.68) | copy-start | bytes 393220
  1853.7 145.2 %slice-start = ((s8[5767168]{0:T(1024)(128)(4,1)}), s8[1572864]{0:T(1024)(128)(4,1)S(1)}, s32[]{:S(2)}) async-start(s8[5767168]{0:T(1024)(128)(4,1)} %bitcast.426), calls=%async_computation.33 | async-start | bytes 3145728
  2009.0 164.7 %copy-start.102 = (f32[16,256]{1,0:T(8,128)S(1)}, f32[16,256]{1,0:T(8,128)}, u32[]{:S(2)}) copy-start(f32[16,256]{1,0:T(8,128)} %get-tuple-element.377) | copy-start | bytes 49156
  (135 other events, 1574.2 us)
Sparse Core Ops, SparseCore 0:
  59.7 67.4 all-reduce.15
  130.7 206.4 reduce-scatter.15
  357.7 88.8 reduce-scatter.17
  451.5 69.8 all-reduce.25
  523.3 48.9 all-gather.9
  575.6 67.7 all-reduce.17
  647.3 372.8 reduce-scatter.19
  1032.6 68.4 all-reduce.19
  1103.2 163.2 all-gather.11
  1301.1 46.7 all-gather.13
  1374.5 68.6 all-reduce.21
  1445.3 97.7 all-gather.15
  1551.7 68.3 all-reduce.23
  1623.6 88.1 reduce-scatter.21
  1715.1 65.2 reduce-scatter.35
  1783.6 64.5 reduce-scatter.33
  1853.7 32.6 all-reduce.27
  1889.4 56.1 reduce-scatter.31
  1948.8 53.9 reduce-scatter.29
  2005.7 53.9 reduce-scatter.27
  2062.8 53.8 reduce-scatter.25
  2119.9 53.8 reduce-scatter.23
where the time goes:
time: 2190 us; the launch traced here: 2180 us
  waiting for transfers between devices  1560 us (71%)
  matrix products  236 us (11%)
  blocking collectives  227 us (10%)
  local copies, waits for them, and re-layouts  70 us (3%)
  other arithmetic  52.8 us (2%)
  between operations  25.9 us (1%)
    reduce_scatter x2, waiting for transfers between devices, project_in(): lax.psum_scatter(partial_term(jnp.int32(0), members * column_count * lax....  587 us
    all_gather x2, waiting for transfers between devices, project_in_back(): return gradient_adder(kept, lax.all_gather(grads, 'mp', axis=1, tiled=True))  259 us
    psum x5, waiting for transfers between devices, rank_total(): return lax.psum(values, 'mp')  229 us
    unnamed x24, waiting for transfers between devices  109 us
    reduce_scatter x1, waiting for transfers between devices, project_down(): lax.psum_scatter(partial_term(jnp.int32(0), column_count * lax.axis_size(...  89.8 us
    psum x2, blocking collectives, rank_total(): return lax.psum(values, 'mp')  72.5 us
    psum x1, waiting for transfers between devices, row_total(): return lax.psum(jnp.sum(values, axis=0), 'mp')  61.1 us
    psum x2, blocking collectives, row_total(): return lax.psum(jnp.sum(values, axis=0), 'mp')  58 us
  transfers between devices with their start and end apart: 22, of which 20 were waited for; matrix products, arithmetic and copies ran while one was open for 12% of the time, Pallas kernels for 0%

commit v1 on v0

v1 whole, which is shorter than its diff:
```python
import jax
import jax.numpy as jnp
from jax import lax
from jax.experimental import pallas as pl
from jax.experimental.pallas import tpu as pltpu
from jax.sharding import PartitionSpec as P

HD = 128
R = 16
ALPHA = 32
SCALE = ALPHA / R
EPS = 1e-05
THETA = 10000.0
NEGATIVE = -1e30
PLANES = 4
CORES = 2
LOW = jnp.bfloat16
F32 = jnp.float32


def swap(values, offset, axis):
    count = lax.axis_size(axis)
    return lax.ppermute(values, axis, [(place, place ^ offset) for place in range(count)])


def gather(chunk):
    count = lax.axis_size("mp")
    inner = count // PLANES
    got = [None] * count
    got[0] = chunk
    for a in range(1, PLANES):
        got[a * inner] = swap(chunk, a * inner, "mp")
    for a in range(PLANES):
        for b in range(1, inner):
            got[a * inner + b] = swap(got[a * inner], b, "mp")
    return got


def total_over(values, axis):
    offset = 1
    while offset < lax.axis_size(axis):
        values = values + swap(values, offset, axis)
        offset *= 2
    return values


def small_gather(chunk):
    count = lax.axis_size("mp")
    inner = count // PLANES
    held = jnp.stack([chunk] + [swap(chunk, a * inner, "mp") for a in range(1, PLANES)])
    sides = [held] + [swap(held, b, "mp") for b in range(1, inner)]
    return jnp.concatenate([sides[k % inner][k // inner] for k in range(count)], axis=1)


def small_scatter(bundles):
    inner = len(bundles)
    held = bundles[0].astype(F32)
    for b in range(1, inner):
        held = held + swap(bundles[b], b, "mp").astype(F32)
    final = held[0]
    for a in range(1, PLANES):
        sent = held[a].astype(LOW)
        final = final + swap(sent, a * inner, "mp").astype(F32)
    return final


def total_relative(values):
    count = values.shape[0]
    offset = 1
    while offset < count:
        turned = jnp.stack([values[k ^ offset] for k in range(count)])
        values = values + swap(turned, offset, "mp")
        offset *= 2
    return values


def dot(left_part, right_part, left_dim=1, right_dim=0):
    return lax.dot_general(
        left_part,
        right_part,
        (((left_dim,), (right_dim,)), ((), ())),
        preferred_element_type=F32,
    )


def split(values):
    high = values.astype(LOW)
    return high, (values - high.astype(F32)).astype(LOW)


def split_rows(values):
    high = lax.reduce_precision(values, 8, 7)
    return jnp.concatenate([high, values - high], axis=0).astype(LOW)


def round_up(size):
    return -(-size // 128) * 128


def pad_to(values, size, axis):
    if values.shape[axis] == size:
        return values
    widths = [(0, 0)] * values.ndim
    widths[axis] = (0, size - values.shape[axis])
    return jnp.pad(values, widths)


def kernel(body, outs, *operands, scalars=None):
    specs = [pl.BlockSpec(memory_space=pltpu.VMEM)] * len(operands)
    if scalars is not None:
        specs = [pl.BlockSpec(memory_space=pltpu.SMEM)] + specs
        operands = (scalars,) + operands
    return pl.pallas_call(
        body,
        out_shape=tuple(jax.ShapeDtypeStruct(shape, kind) for shape, kind in outs),
        in_specs=specs,
    )(*operands)


def by_rows(body, steps, chunks, rowed, summed_outs, across, outs, *operands):
    def spec(shape, by_block):
        if by_block:
            return pl.BlockSpec((shape[0] // steps, shape[1]), lambda i: (i, 0))
        return pl.BlockSpec(shape, lambda i: (0, 0))

    out_specs = [spec(shape, slot not in summed_outs) for slot, (shape, _) in enumerate(outs)]
    if across is not None:
        shape = outs[across][0]
        out_specs[across] = pl.BlockSpec((shape[0], shape[1] // steps), lambda i: (0, i))
    return pl.pallas_call(
        body,
        grid=(steps,),
        in_specs=[
            spec(operand.shape, slot < chunks or slot in rowed)
            for slot, operand in enumerate(operands)
        ],
        out_specs=out_specs,
        out_shape=[jax.ShapeDtypeStruct(shape, kind) for shape, kind in outs],
    )(*operands)


def add_low(first, *others):
    def body(*refs):
        total = refs[0][...].astype(F32)
        for ref in refs[1:-1]:
            total = total + ref[...].astype(F32)
        refs[-1][...] = total.astype(LOW)

    return kernel(body, [(first.shape, LOW)], first, *others)[0]


def scatter_pieces(parts):
    count = len(parts)
    inner = count // PLANES
    order = list(range(1, PLANES)) + [0]
    got = {a: [swap(parts[a * inner + b], b, "mp") for b in range(1, inner)] for a in order}
    sent = [swap(add_low(parts[a * inner], *got[a]), a * inner, "mp") for a in order[:-1]]
    return [parts[0]] + got[0] + sent


def summed(refs):
    total = refs[0][...].astype(F32)
    for ref in refs[1:]:
        total = total + ref[...].astype(F32)
    return total


def take_columns(ref, taken, index, width, padded):
    start = index * width
    if width % 128 == 0:
        return ref[taken, pl.ds(pl.multiple_of(start, 128), width)]
    window = round_up(width + 127)
    base = pl.multiple_of(jnp.minimum((start >> 7) << 7, ref.shape[1] - window), 128)
    values = ref[taken, pl.ds(base, window)]
    turn = lax.rem(window - (start - base), window)
    turned = pltpu.roll(values.astype(F32), turn, axis=1)[:, :padded]
    lanes = lax.broadcasted_iota(jnp.int32, turned.shape, 1)
    return jnp.where(lanes < width, turned, 0.0).astype(values.dtype)


def own_factors(rights, magnitudes, width, hidden, padded, scalars):
    def body(place_ref, *refs):
        right_refs, magnitude_refs = refs[:5], refs[5:12]
        place = place_ref[0]
        for members, size, filled, pair_ref in (
            (range(3), width, width, refs[12]),
            (range(3, 5), hidden, padded, refs[13]),
        ):
            half = len(members) * R
            pair_ref[...] = jnp.zeros_like(pair_ref)
            for slot, member in enumerate(members):
                high, rest = split(
                    take_columns(right_refs[member], slice(None), place, size, filled)
                )
                rows = slice(slot * R, (slot + 1) * R)
                lanes = slice(slot * filled, (slot + 1) * filled)
                pair_ref[rows, lanes] = high
                pair_ref[half + slot * R : half + (slot + 1) * R, lanes] = rest
        taken = [
            take_columns(
                ref,
                slice(None),
                place,
                hidden if member in (4, 5) else width,
                padded if member in (4, 5) else width,
            )
            for member, ref in enumerate(magnitude_refs)
        ]
        for slot in range(3):
            refs[14][:, slot * width : (slot + 1) * width] = taken[slot]
        refs[15][:, :padded] = taken[4]
        refs[15][:, padded:] = taken[5]
        refs[16][...] = taken[3]
        refs[17][...] = taken[6]

    return kernel(
        body,
        [
            ((6 * R, 3 * width), LOW),
            ((4 * R, 2 * padded), LOW),
            ((1, 3 * width), F32),
            ((1, 2 * padded), F32),
            ((1, width), F32),
            ((1, width), F32),
        ],
        *[rights[member] for member in (0, 1, 2, 4, 5)],
        *[values[None] for values in magnitudes],
        scalars=scalars,
    )


def gathered_lefts(chunks, tokens):
    width = chunks[0].shape[1]

    def body(*refs):
        left_ref, gain_ref = refs[-2:]
        for k, ref in enumerate(refs[:-2]):
            lanes = slice(k * width, (k + 1) * width)
            left_ref[:, lanes] = ref[tokens : tokens + 6 * R, :]
            gain_ref[:, lanes] = ref[tokens + 6 * R : tokens + 6 * R + 16, :].astype(F32)[1:2]

    total = len(chunks) * width
    outs = [((6 * R, total), LOW), ((1, total), F32)]
    return kernel(body, outs, *chunks)


def cut_blocks(weights, width, padded, scalars):
    count = lax.axis_size("mp")
    members = len(weights)
    rows, _ = weights[0].shape
    part = rows // lax.axis_size("dp")

    def body(place_ref, *refs):
        sources, own_ref, block_refs = refs[:members], refs[members], refs[members + 1 :]
        place = place_ref[0]
        mine = pl.ds(pl.multiple_of(place_ref[1] * part, part), part)

        for slot, ref in enumerate(sources):
            lanes = slice(slot * padded, (slot + 1) * padded)
            own_ref[:, lanes] = take_columns(ref, slice(None), place, width, padded)
            for k in range(1, count):
                block_refs[k - 1][:, lanes] = take_columns(
                    ref, mine, place ^ k, width, padded
                )

    wide = members * padded
    return kernel(
        body, [((rows, wide), LOW)] + [((part, wide), LOW)] * (count - 1), *weights, scalars=scalars
    )


def bundled(blocks):
    def body(*refs):
        for slot, ref in enumerate(refs[:-1]):
            refs[-1][slot] = ref[...]

    shape = (len(blocks),) + blocks[0].shape
    return kernel(body, [(shape, LOW)], *blocks)[0]


def exchanged(blocks):
    bundle = bundled([swap(block, k + 1, "mp") for k, block in enumerate(blocks)])
    pieces = []
    for j in range(0, lax.axis_size("dp"), CORES):
        held = bundle if j == 0 else swap(bundle, j, "dp")
        pieces.append(held)
        pieces += [swap(held, c, "dp") for c in range(1, CORES)]
    return pieces


def thrice(pair, swapped):
    half = pair.shape[0] // 2
    high, rest = pair[:half], pair[half:]
    return jnp.concatenate([high, high, rest] if swapped else [high, rest, high], axis=0)


def assemble(own, pieces, lefts_all, rights_pair, scalars, keep):
    count = lax.axis_size("mp")
    rows, wide = own.shape
    part = pieces[0].shape[1]
    copies = len(pieces)

    def body(place_ref, own_ref, left_ref, right_ref, *refs):
        piece_refs, (weight_ref, full_ref, square_ref) = refs[:copies], refs[copies:]
        k = pl.program_id(0)

        @pl.when(k == 0)
        def _():
            weight_ref[...] = own_ref[...]
            square_ref[...] = jnp.zeros_like(square_ref)

        @pl.when(k > 0)
        def _():
            for j, ref in enumerate(piece_refs):
                at = pl.multiple_of((place_ref[1] ^ j) * part, part)
                weight_ref[pl.ds(at, part), :] = ref[0]

        full = weight_ref[...].astype(F32) + dot(
            thrice(left_ref[...], False), thrice(right_ref[...], True), 0, 0
        )
        full_ref[...] = full.astype(LOW)
        square_ref[...] += jnp.sum(full * full, axis=0, keepdims=True)

    whole = lambda k: (0, 0)

    def body_alone(*refs):
        body(*refs[: 4 + copies], refs[-1], *refs[4 + copies : -1])

    return pl.pallas_call(
        body if keep else body_alone,
        scratch_shapes=[] if keep else [pltpu.VMEM((rows, wide), LOW)],
        grid=(count,),
        in_specs=[
            pl.BlockSpec(memory_space=pltpu.SMEM),
            pl.BlockSpec((rows, wide), whole),
            pl.BlockSpec((lefts_all.shape[0], rows), lambda k: (0, k)),
            pl.BlockSpec(rights_pair.shape, whole),
        ]
        + [pl.BlockSpec((1, part, wide), lambda k: (jnp.maximum(k - 1, 0), 0, 0))] * len(pieces),
        out_specs=[pl.BlockSpec((rows, wide), lambda k: (k, 0))] * (2 if keep else 1)
        + [pl.BlockSpec((1, wide), whole)],
        out_shape=[jax.ShapeDtypeStruct((count * rows, wide), LOW)] * (2 if keep else 1)
        + [jax.ShapeDtypeStruct((1, wide), F32)],
    )(scalars, own, lefts_all, rights_pair, *pieces)


def row_block(weight, left_pair, right, magnitude, width, rows_padded, scalars):
    count = lax.axis_size("mp")
    rows, total = weight.shape

    def body(
        place_ref,
        weight_ref,
        left_ref,
        right_ref,
        magnitude_ref,
        full_ref,
        high_ref,
        square_ref,
        moved_ref,
        *cross_refs,
    ):
        lefts = thrice(left_ref[...], False)
        for k in range(count):
            at = pl.ds(pl.multiple_of((place_ref[0] ^ k) * width, width), width)
            lanes = slice(k * width, (k + 1) * width)
            values = weight_ref[:, at]
            if rows < rows_padded:
                fill = jnp.zeros((rows_padded - rows, width), LOW)
                values = jnp.concatenate([values, fill], axis=0)
            high, rest = split(right_ref[:, at])
            pair = jnp.concatenate([high, rest], axis=0)
            high_ref[:, lanes] = high
            moved_ref[:, lanes] = magnitude_ref[:, at]
            full = values.astype(F32) + dot(lefts, thrice(pair, True), 0, 0)
            low = full.astype(LOW)
            full_ref[:, lanes] = low
            square_ref[:, lanes] = jnp.sum(full * full, axis=0, keepdims=True)
            a, b = divmod(k, count // PLANES)
            cross_refs[b][a] = dot(left_ref[:R, :], low).astype(LOW)

    return kernel(
        body,
        [
            ((rows_padded, total), LOW),
            ((R, total), LOW),
            ((1, total), F32),
            ((1, total), F32),
        ]
        + [((PLANES, R, width), LOW)] * (count // PLANES),
        weight,
        left_pair,
        right,
        magnitude,
        scalars=scalars,
    )


def inner_product(inputs, lefts_pair):
    half = lefts_pair.shape[0] // 2
    return dot(inputs, lefts_pair[:half], 1, 1) + dot(inputs, lefts_pair[half:], 1, 1)


def adapter_term(inner, rights_pair):
    half = rights_pair.shape[0] // 2
    high, rest = split(inner)
    return (
        dot(high, rights_pair[:half]) + dot(rest, rights_pair[:half]) + dot(high, rights_pair[half:])
    )


def halves_turned(values):
    return pltpu.roll(values, HD // 2, axis=1)


def allowed_pairs(seg_rows, seg_cols):
    length = seg_rows.shape[0]
    row_at = lax.broadcasted_iota(jnp.int32, (length, length), 0)
    col_at = lax.broadcasted_iota(jnp.int32, (length, length), 1)
    return (seg_rows == seg_cols) & (col_at <= row_at)


def lane_sums_as_row(values):
    folded = values[:, :128]
    for at in range(128, values.shape[1], 128):
        folded = folded + values[:, at : at + 128]
    return jnp.sum(folded.T, axis=0, keepdims=True)


def row_as_columns(row, lanes):
    return jnp.broadcast_to(row, (lanes, row.shape[1])).T


def put_chunks(refs, values, width):
    for k, ref in enumerate(refs):
        ref[...] = values[:, k * width : (k + 1) * width].astype(LOW)


def first_half_body(*refs):
    count = (len(refs) - 20) // 2
    chunk_refs = refs[:count]
    (
        weight_ref,
        square_ref,
        magnitude_ref,
        left_ref,
        right_ref,
        cos_ref,
        sin_ref,
        segr_ref,
        segc_ref,
        out_full_ref,
    ) = refs[count : count + 10]
    (
        normed_ref,
        proj_ref,
        inner_ref,
        q_ref,
        k_ref,
        v_ref,
        mix_ref,
        lse_ref,
        inverse_ref,
        factor_ref,
    ) = refs[count + 10 : count + 20]
    part_refs = refs[count + 20 :]
    tokens, width = mix_ref.shape
    heads = width // HD
    gain_at = chunk_refs[0].shape[0] - 16
    squares = jnp.zeros((tokens, width), F32)
    for ref in chunk_refs:
        values = ref[:tokens, :].astype(F32)
        squares = squares + values * values
    inverse = lax.rsqrt(jnp.sum(squares, axis=1, keepdims=True) / (width * count) + EPS)
    inverse_ref[...] = inverse
    for k, ref in enumerate(chunk_refs):
        gain = ref[gain_at : gain_at + 16, :].astype(F32)[:1]
        values = ref[:tokens, :].astype(F32)
        normed_ref[:, k * width : (k + 1) * width] = (values * inverse * gain).astype(LOW)
    normed = normed_ref[...]
    inner = inner_product(normed, left_ref[...])
    inner_ref[...] = inner
    proj_ref[...] = dot(normed, weight_ref[...]) + adapter_term(inner, right_ref[...])
    factor_ref[...] = magnitude_ref[...] / jnp.sqrt(square_ref[...])
    cosine = cos_ref[...]
    sine = sin_ref[...]
    allowed = allowed_pairs(segr_ref[...], segc_ref[...])
    for head in range(heads):
        at = head * HD
        taken = []
        for member in range(3):
            lanes = slice(member * width + at, member * width + at + HD)
            taken.append(proj_ref[:, lanes] * factor_ref[:, lanes])
        queries = (taken[0] * cosine + halves_turned(taken[0]) * sine).astype(LOW)
        keys = (taken[1] * cosine + halves_turned(taken[1]) * sine).astype(LOW)
        values = taken[2].astype(LOW)
        logits = jnp.where(allowed, dot(queries, keys, 1, 1) * HD ** (-0.5), NEGATIVE)
        highest = jnp.max(logits, axis=1, keepdims=True)
        powers = jnp.exp(logits - highest)
        totals = jnp.sum(powers, axis=1, keepdims=True)
        probs_low = (powers / totals).astype(LOW)
        mix_ref[:, at : at + HD] = dot(probs_low, values).astype(LOW)
        q_ref[:, at : at + HD] = queries
        k_ref[:, at : at + HD] = keys
        v_ref[:, at : at + HD] = values
        lse_ref[:, head : head + 1] = highest + jnp.log(totals)
    put_chunks(part_refs, dot(mix_ref[...], out_full_ref[...]), width)


def feed_forward_body(*refs):
    count = (len(refs) - 11) // 2
    chunk_refs = refs[:count]
    (
        gain_ref,
        full_ref,
        square_ref,
        magnitude_ref,
        dact_ref,
    ) = refs[count : count + 5]
    scaled_ref, inverse_ref, act_ref, low_ref, scale_ref, token_ref = refs[count + 5 : count + 11]
    part_refs = refs[count + 11 :]
    width = chunk_refs[0].shape[1]
    hidden = act_ref.shape[1]
    squares = jnp.zeros(chunk_refs[0].shape, F32)
    for k, ref in enumerate(chunk_refs):
        lanes = slice(k * width, (k + 1) * width)
        values = ref[...]
        scaled_ref[:, lanes] = values
        raw = values.astype(F32) * (1.0 / gain_ref[:, lanes])
        squares = squares + raw * raw
    inverse = lax.rsqrt(jnp.sum(squares, axis=1, keepdims=True) / (width * count) + EPS)
    inverse_ref[...] = inverse
    proj = dot(scaled_ref[...], full_ref[...])
    factor = magnitude_ref[...] / jnp.sqrt(jnp.where(square_ref[...] == 0.0, 1.0, square_ref[...]))
    gate_factor, up_factor = factor[:, :hidden], factor[:, hidden:]
    gate_proj, up_proj = proj[:, :hidden], proj[:, hidden:]
    gate_shaped = gate_proj * inverse
    up_shaped = up_proj * inverse
    gate = gate_shaped * gate_factor
    upper = up_shaped * up_factor
    sigma = 1.0 / (1.0 + jnp.exp(-gate))
    silu = gate * sigma
    act_ref[...] = (silu * upper).astype(LOW)
    grads = dact_ref[...]
    grad_gate = grads * upper * (sigma * (1.0 + gate * (1.0 - sigma)))
    grad_up = grads * silu

    @pl.when(pl.program_id(0) == 0)
    def _():
        scale_ref[...] = jnp.zeros_like(scale_ref)

    scale_ref[:, :hidden] += jnp.sum(grad_gate * gate_shaped, axis=0, keepdims=True)
    scale_ref[:, hidden:] += jnp.sum(grad_up * up_shaped, axis=0, keepdims=True)
    low_gate = (grad_gate * gate_factor).astype(LOW)
    low_up = (grad_up * up_factor).astype(LOW)
    low_ref[:, :hidden] = low_gate
    low_ref[:, hidden:] = low_up
    token_ref[...] = lane_sums_as_row(
        low_gate.astype(F32) * gate_proj + low_up.astype(F32) * up_proj
    )
    for k, ref in enumerate(part_refs):
        ref[...] = dot(low_ref[...], full_ref[k * width : (k + 1) * width, :], 1, 1).astype(LOW)


def down_body(act_ref, full_ref, *part_refs):
    put_chunks(part_refs, dot(act_ref[...], full_ref[...]), part_refs[0].shape[1])


def down_grad_body(*refs):
    chunk_refs = refs[:-6]
    square_ref, magnitude_ref, full_ref, left_ref, grad_ref, dact_ref = refs[-6:]
    width = chunk_refs[0].shape[1]
    tokens = grad_ref.shape[0]
    factor = magnitude_ref[...] / jnp.sqrt(square_ref[...])
    for k, ref in enumerate(chunk_refs):
        lanes = slice(k * width, (k + 1) * width)
        grad_ref[:, lanes] = (ref[:tokens, :].astype(F32) * factor[:, lanes]).astype(LOW)
        left_ref[:, lanes] = ref[tokens:, :]
    dact_ref[...] = dot(grad_ref[...], full_ref[...], 1, 1)


def middle_body(*refs):
    piece_refs = refs[:-6]
    token_ref, gain_ref, factor_ref, shaped_ref, middle_ref, chunk_ref = refs[-6:]
    shaped = summed(piece_refs)
    shaped_ref[...] = shaped
    middle = token_ref[...].astype(F32) + shaped * factor_ref[...]
    middle_ref[...] = middle
    chunk_ref[...] = (middle * gain_ref[...]).astype(LOW)


def result_body(*refs):
    piece_refs = refs[:-5]
    middle_ref, cotangent_ref, factor_ref, out_ref, scale_ref = refs[-5:]
    shaped = summed(piece_refs)
    out_ref[...] = (middle_ref[...] + shaped * factor_ref[...]).astype(LOW)
    scale_ref[...] = jnp.sum(cotangent_ref[...].astype(F32) * shaped, axis=0, keepdims=True)


def grad_middle_body(*refs):
    piece_refs = refs[:-10]
    (
        cotangent_ref,
        middle_ref,
        inverse_ref,
        gain_ref,
        token_ref,
        factor_ref,
        shaped_ref,
        grad_ref,
        low_ref,
        scale_ref,
    ) = refs[-10:]
    _, width = middle_ref.shape
    inverse = inverse_ref[...]
    token_sums = row_as_columns(token_ref[...], width)
    model_width = width * lax.axis_size("mp")
    grads = (
        cotangent_ref[...].astype(F32)
        + inverse * gain_ref[...] * summed(piece_refs)
        - middle_ref[...] * (inverse * inverse * inverse / model_width * token_sums)
    )
    grad_ref[...] = grads
    low_ref[...] = (grads * factor_ref[...]).astype(LOW)
    scale_ref[...] = jnp.sum(grads * shaped_ref[...], axis=0, keepdims=True)


def input_grad_body(*refs):
    piece_refs = refs[:-6]
    grad_ref, token_ref, inverse_ref, gain_ref, sum_ref, out_ref = refs[-6:]
    _, width = grad_ref.shape
    inverse = inverse_ref[...]
    token_sums = row_as_columns(sum_ref[...], width)
    model_width = width * lax.axis_size("mp")
    out_ref[...] = (
        grad_ref[...]
        + inverse * gain_ref[...] * summed(piece_refs)
        - token_ref[...].astype(F32) * (inverse * inverse / model_width * token_sums)
    )


def second_half_body(*refs):
    count = (len(refs) - 16) // 2
    chunk_refs = refs[:count]
    (
        out_full_ref,
        q_ref,
        k_ref,
        v_ref,
        lse_ref,
        proj_ref,
        factor_ref,
        cos_ref,
        sin_ref,
        segr_ref,
        segc_ref,
        full_ref,
    ) = refs[count : count + 12]
    all_ref, g_ref, scale_ref, token_ref = refs[count + 12 : count + 16]
    part_refs = refs[count + 16 :]
    tokens, width = chunk_refs[0].shape
    heads = width // HD
    for k, ref in enumerate(chunk_refs):
        all_ref[:, k * width : (k + 1) * width] = ref[...]
    mixed_grads = dot(all_ref[...], out_full_ref[...], 1, 1).astype(LOW)
    cosine = cos_ref[...]
    sine = sin_ref[...]
    allowed = allowed_pairs(segr_ref[...], segc_ref[...])
    token_total = jnp.zeros((tokens, HD), F32)
    for head in range(heads):
        at = head * HD
        queries = q_ref[:, at : at + HD]
        keys = k_ref[:, at : at + HD]
        values = v_ref[:, at : at + HD]
        mixed_grad = mixed_grads[:, at : at + HD]
        logits = jnp.where(allowed, dot(queries, keys, 1, 1) * HD ** (-0.5), NEGATIVE)
        probs = jnp.exp(logits - lse_ref[:, head : head + 1])
        prob_grad = dot(mixed_grad, values, 1, 1)
        delta = jnp.sum(prob_grad * probs, axis=1, keepdims=True)
        raw_grad = (probs * (prob_grad - delta) * HD ** (-0.5)).astype(LOW)
        query_grad = dot(raw_grad, keys)
        key_grad = dot(raw_grad, queries, 0, 0)
        value_grad = dot(probs.astype(LOW), mixed_grad, 0, 0)
        grads = (
            query_grad * cosine - halves_turned(query_grad) * sine,
            key_grad * cosine - halves_turned(key_grad) * sine,
            value_grad,
        )
        for member in range(3):
            lanes = slice(member * width + at, member * width + at + HD)
            shaped = proj_ref[:, lanes]
            lowered = (grads[member] * factor_ref[:, lanes]).astype(LOW)
            g_ref[:, lanes] = lowered
            scale_ref[:, lanes] = jnp.sum(grads[member] * shaped, axis=0, keepdims=True)
            token_total = token_total + lowered.astype(F32) * shaped
    token_ref[...] = lane_sums_as_row(token_total)
    for k, ref in enumerate(part_refs):
        ref[...] = dot(g_ref[...], full_ref[k * width : (k + 1) * width, :], 1, 1).astype(LOW)


def put_bundles(refs, rows, values):
    inner = len(refs)
    width = refs[0].shape[2]
    for b, ref in enumerate(refs):
        for a in range(PLANES):
            at = (a * inner + b) * width
            ref[a, rows, :] = values[:, at : at + width].astype(LOW)


def negative_ratio(scale, magnitude, square):
    norm = jnp.sqrt(jnp.where(square == 0.0, 1.0, square))
    return -scale * magnitude / (norm * norm * norm)


def column_adapters(
    low_grad, inputs, inner, inverse, full, square, magnitude, scale, lefts, rights, members
):
    half = rights.shape[0] // 2
    high = rights[:half]
    ratio = negative_ratio(scale, magnitude, square)
    rank = dot(low_grad, high, 1, 1)
    if inverse is not None:
        rank = rank * inverse
        inner = inner * inverse
    left_part = dot(rank.astype(LOW), inputs, 0, 0) + dot(
        (high.astype(F32) * ratio).astype(LOW), full, 1, 1
    )
    right_part = dot(inner.astype(LOW), low_grad, 0, 0) + ratio * dot(lefts[:half], full)
    size = low_grad.shape[1] // members
    rights_out = [
        right_part[slot * R : (slot + 1) * R, slot * size : (slot + 1) * size]
        for slot in range(members)
    ]
    return SCALE * left_part, rights_out


def two_adapters_body(
    low_ref,
    scaled_ref,
    inverse_ref,
    full_ref,
    square_ref,
    magnitude_ref,
    scale_ref,
    left_ref,
    right_ref,
    broad_ref,
    *bundle_refs,
):
    hidden = broad_ref.shape[1]
    left_part, rights_out = column_adapters(
        low_ref[...],
        scaled_ref[...],
        inner_product(scaled_ref[...], left_ref[...]),
        inverse_ref[...],
        full_ref[...],
        square_ref[...],
        magnitude_ref[...],
        scale_ref[...],
        left_ref[...],
        right_ref[...],
        2,
    )
    put_bundles(bundle_refs, slice(None), left_part)
    broad_ref[:R, :] = rights_out[0]
    broad_ref[R : 2 * R, :] = rights_out[1]
    broad_ref[2 * R : 2 * R + 1, :] = scale_ref[:, :hidden]
    broad_ref[2 * R + 1 : 2 * R + 2, :] = scale_ref[:, hidden:]
    broad_ref[2 * R + 2 :, :] = jnp.zeros((6, hidden), F32)


def row_adapters(grads, inputs, high, left_rows):
    rank = dot(grads, high, 1, 1)
    left_part = SCALE * dot(rank.astype(LOW), inputs, 0, 0)
    inner = dot(inputs, left_rows, 1, 1)
    return left_part, dot(inner.astype(LOW), grads, 0, 0)


def ratio_adapters_body(
    out_high_ref, out_full_ref, down_high_ref, down_full_ref, ratio_ref, rows_ref
):
    width = rows_ref.shape[1]
    for slot, (high_ref, full_ref) in enumerate(
        ((out_high_ref, out_full_ref), (down_high_ref, down_full_ref))
    ):
        scaled = (high_ref[...].astype(F32) * ratio_ref[slot : slot + 1, :]).astype(LOW)
        part = SCALE * dot(scaled, full_ref[...], 1, 1)
        for first in range(0, part.shape[1], width):
            at = slot * R + first // width * R
            rows_ref[at : at + R, :] = part[:, first : first + width]


def end_adapters_body(*refs):
    (
        low_ref,
        normed_ref,
        inner_ref,
        full_ref,
        square_ref,
        magnitude_ref,
        scale_ref,
        left_ref,
        right_ref,
        gout_ref,
        mixed_ref,
        out_high_ref,
        out_left_ref,
        gdown_ref,
        act_ref,
        down_high_ref,
        down_left_ref,
    ) = refs[:17]
    inner = (len(refs) - 18) // 4
    moved_refs, rows_ref, bundle_refs = refs[17:-inner - 1], refs[-inner - 1], refs[-inner:]
    for b, ref in enumerate(bundle_refs):
        ref[:, 5 * R : 7 * R, :] = moved_refs[b][...]
        ref[:, 7 * R : 8 * R, :] = moved_refs[inner + b][...]
        ref[:, 8 * R :, :] = moved_refs[2 * inner + b][...]
    width = rows_ref.shape[1]
    left_part, rights_out = column_adapters(
        low_ref[...],
        normed_ref[...],
        inner_ref[...],
        None,
        full_ref[...],
        square_ref[...],
        magnitude_ref[...],
        scale_ref[...],
        left_ref[...],
        right_ref[...],
        3,
    )
    put_bundles(bundle_refs, slice(0, 3 * R), left_part)
    left_out, right_out = row_adapters(
        gout_ref[...],
        mixed_ref[...],
        out_high_ref[...],
        out_left_ref[:R, :],
    )
    put_bundles(bundle_refs, slice(3 * R, 4 * R), right_out)
    left_down, right_down = row_adapters(
        gdown_ref[...],
        act_ref[...],
        down_high_ref[...],
        down_left_ref[:R, :],
    )
    put_bundles(bundle_refs, slice(4 * R, 5 * R), right_down)
    at = 0
    for values in rights_out + [left_out]:
        rows_ref[at : at + R, :] = values
        at += R
    for first in range(0, left_down.shape[1], width):
        rows_ref[at : at + R, :] = left_down[:, first : first + width]
        at += R
    for slot in range(3):
        rows_ref[at + slot : at + slot + 1, :] = scale_ref[:, slot * width : (slot + 1) * width]
    rows_ref[at + 3 : at + 8, :] = jnp.zeros((5, width), F32)


def statistics_body(*refs):
    out_ref = refs[-1]
    rows = lax.broadcasted_iota(jnp.int32, out_ref.shape, 0)
    lanes = lax.broadcasted_iota(jnp.int32, out_ref.shape, 1)
    table = jnp.zeros(out_ref.shape, F32)
    member = 0
    for slot, members in enumerate((3, 1, 2, 1)):
        norms = jnp.sqrt(refs[2 * slot][...])
        drifts = refs[2 * slot + 1][...] - norms
        size = norms.shape[1] // members
        for part in range(members):
            taken = slice(part * size, (part + 1) * size)
            norm, drift = norms[:, taken], drifts[:, taken]
            first = jnp.sum(drift * drift, axis=1, keepdims=True)
            second = jnp.sum(norm, axis=1, keepdims=True)
            table = jnp.where(rows == member, jnp.where(lanes == 0, first, second), table)
            member += 1
    out_ref[...] = table


def on_device(
    tokens,
    cotangent,
    segment_ids,
    attention_gain,
    feedforward_gain,
    *parameters,
):
    count = lax.axis_size("mp")
    inner_count = count // PLANES
    place = lax.axis_index("mp")
    scalars = jnp.stack([place, lax.axis_index("dp")]).astype(jnp.int32)
    weights = parameters[:7]
    lefts = parameters[7::3]
    rights = parameters[8::3]
    magnitudes = parameters[9::3]
    token_count, width = tokens.shape
    hidden = weights[4].shape[1] // count
    hidden_padded = round_up(hidden)
    widths = [weight.shape[1] // count for weight in weights]
    chunk_shape = (token_count, width)
    rights_one, rights_two, magnitude_one, magnitude_two, magnitude_out, magnitude_down = (
        own_factors(rights, magnitudes, width, hidden, hidden_padded, scalars)
    )

    def lefts_of(members):
        return split_rows(
            SCALE * jnp.concatenate([lefts[member].T for member in members], axis=0)
        )

    own_one, *blocks_one = cut_blocks(weights[:3], width, width, scalars)
    extended = jnp.concatenate(
        [
            tokens,
            lefts_of((0, 1, 2)),
            attention_gain[None],
            feedforward_gain[None],
            jnp.zeros((14, width), LOW),
        ],
        axis=0,
    )
    token_chunks = gather(extended)
    pieces_one = exchanged(blocks_one)
    lefts_one, gain_two_all = gathered_lefts(token_chunks, token_count)
    weight_one, full_one, squares_one = assemble(
        own_one, pieces_one, lefts_one, rights_one, scalars, True
    )

    length = segment_ids.shape[1]
    key_index = jnp.arange(length, dtype=jnp.int32)
    segments = segment_ids[0]
    change = jnp.concatenate(
        [jnp.ones((1,), jnp.int32), (segments[1:] != segments[:-1]).astype(jnp.int32)]
    )
    places = (key_index - lax.cummax(key_index * change, axis=0)).astype(F32)
    half = HD // 2
    freqs = THETA ** (-2.0 * jnp.arange(half, dtype=F32) / HD)
    angles = places[:, None] * freqs[None, :]
    cosine = jnp.cos(angles)
    sine = jnp.sin(angles)
    cosine = jnp.concatenate([cosine, cosine], axis=1)
    sine = jnp.concatenate([-sine, sine], axis=1)
    seg_rows = segments[:, None]
    seg_cols = segments[None, :]

    left_out = lefts_of((3,))
    left_down = pad_to(lefts_of((6,)), hidden_padded, 1)
    full_out, high_out, squares_out, _, *cross_out = row_block(
        weights[3], left_out, rights[3], magnitudes[3][None], width, width, scalars
    )
    full_down, high_down, squares_down, magnitude_down_all, *cross_down = row_block(
        weights[6], left_down, rights[6], magnitudes[6][None], width, hidden_padded, scalars
    )
    squares_all = total_relative(
        jnp.concatenate([squares_out, squares_down], axis=0)
        .reshape(2, count, width)
        .transpose(1, 0, 2),
    )
    square_out, square_down = squares_all[0, :1], squares_all[0, 1:]
    square_down_all = squares_all[:, 1].reshape(1, count * width)
    factor_out = magnitude_out / jnp.sqrt(square_out)
    factor_down = magnitude_down / jnp.sqrt(square_down)

    heads = width // HD
    (
        normed_one,
        proj_one,
        inner_one,
        queries,
        keys,
        values,
        mixed,
        log_totals,
        inverse_one,
        factor_one,
        *parts_out,
    ) = kernel(
        first_half_body,
        [
            ((token_count, count * width), LOW),
            ((token_count, 3 * width), F32),
            ((token_count, 3 * R), F32),
        ]
        + [(chunk_shape, LOW)] * 4
        + [((token_count, heads), F32), ((token_count, 1), F32), ((1, 3 * width), F32)]
        + [(chunk_shape, LOW)] * count,
        *token_chunks,
        weight_one,
        squares_one,
        magnitude_one,
        lefts_one,
        rights_one,
        cosine,
        sine,
        seg_rows,
        seg_cols,
        full_out,
    )
    gain_one = attention_gain.astype(F32)[None]
    gain_two = feedforward_gain.astype(F32)[None]
    shaped_out, middle, chunk_two = kernel(
        middle_body,
        [(chunk_shape, F32), (chunk_shape, F32), (chunk_shape, LOW)],
        *scatter_pieces(parts_out),
        tokens,
        gain_two,
        factor_out,
    )

    cotangent_chunks = gather(jnp.concatenate([cotangent, lefts_of((4, 5))], axis=0))
    lefts_two, grad_down_all, grad_activated = kernel(
        down_grad_body,
        [
            ((4 * R, count * width), LOW),
            ((token_count, count * width), LOW),
            ((token_count, hidden_padded), F32),
        ],
        *cotangent_chunks,
        square_down_all,
        magnitude_down_all,
        full_down,
    )
    own_two, *blocks_two = cut_blocks(weights[4:6], hidden, hidden_padded, scalars)
    full_two, squares_two = assemble(
        own_two, exchanged(blocks_two), lefts_two, rights_two, scalars, False
    )

    scaled_two, inverse_two, activated, low_two, scale_two, token_two, *parts_two = by_rows(
        feed_forward_body,
        2,
        count,
        (count + 4,),
        (4,),
        5,
        [
            ((token_count, count * width), LOW),
            ((token_count, 1), F32),
            ((token_count, hidden_padded), LOW),
            ((token_count, 2 * hidden_padded), LOW),
            ((1, 2 * hidden_padded), F32),
            ((1, token_count), F32),
        ]
        + [(chunk_shape, LOW)] * count,
        *gather(chunk_two),
        gain_two_all,
        full_two,
        squares_two,
        magnitude_two,
        grad_activated,
    )
    token_two = total_over(token_two, "mp")
    grad_middle, grad_out, scale_out = kernel(
        grad_middle_body,
        [(chunk_shape, F32), (chunk_shape, LOW), ((1, width), F32)],
        *scatter_pieces(parts_two),
        cotangent,
        middle,
        inverse_two,
        gain_two,
        token_two,
        factor_out,
        shaped_out,
    )
    parts_down = by_rows(
        down_body, 2, 1, (), (), None, [(chunk_shape, LOW)] * count, activated, full_down
    )
    layer_out, scale_down = kernel(
        result_body,
        [(chunk_shape, LOW), ((1, width), F32)],
        *scatter_pieces(parts_down),
        middle,
        cotangent,
        factor_down,
    )

    grad_out_all, low_one, scale_one, token_one, *parts_one = kernel(
        second_half_body,
        [
            ((token_count, count * width), LOW),
            ((token_count, 3 * width), LOW),
            ((1, 3 * width), F32),
            ((1, token_count), F32),
        ]
        + [(chunk_shape, LOW)] * count,
        *gather(grad_out),
        full_out,
        queries,
        keys,
        values,
        log_totals,
        proj_one,
        factor_one,
        cosine,
        sine,
        seg_rows,
        seg_cols,
        full_one,
    )
    token_one = total_over(token_one, "mp")
    (input_gradient,) = kernel(
        input_grad_body,
        [(chunk_shape, F32)],
        *scatter_pieces(parts_one),
        grad_middle,
        tokens,
        inverse_one,
        gain_one,
        token_one,
    )

    broad, *bundles = kernel(
        two_adapters_body,
        [((2 * R + 8, hidden_padded), F32)] + [((PLANES, 2 * R, width), LOW)] * inner_count,
        low_two,
        scaled_two,
        inverse_two,
        full_two,
        squares_two,
        magnitude_two,
        scale_two,
        lefts_two,
        rights_two,
    )
    broad = total_over(broad, "dp")

    ratio_rows = small_gather(
        jnp.concatenate(
            [
                negative_ratio(scale_out, magnitude_out, square_out),
                negative_ratio(scale_down, magnitude_down, square_down),
            ],
            axis=0,
        ),
    )
    slabs = hidden_padded // width
    rows_end, *bundles_end = kernel(
        end_adapters_body,
        [(((4 + slabs) * R + 8, width), F32)] + [((PLANES, 9 * R, width), LOW)] * inner_count,
        low_one,
        normed_one,
        inner_one,
        full_one,
        squares_one,
        magnitude_one,
        scale_one,
        lefts_one,
        rights_one,
        grad_out_all,
        mixed,
        high_out,
        left_out,
        grad_down_all,
        activated,
        high_down,
        left_down,
        *bundles,
        *cross_out,
        *cross_down,
    )
    spread = small_scatter(bundles_end)
    crossed = spread[7 * R :]
    (rows_ratio,) = kernel(
        ratio_adapters_body,
        [(((1 + slabs) * R, width), F32)],
        high_out,
        full_out,
        high_down,
        full_down,
        ratio_rows,
    )
    last = total_over(
        jnp.concatenate(
            [
                spread[: 7 * R],
                rows_end[: 3 * R],
                rows_end[3 * R : (4 + slabs) * R] + rows_ratio,
                rows_end[(4 + slabs) * R :][:3],
                scale_out,
                scale_down,
                jnp.zeros((3, width), F32),
            ],
            axis=0,
        ),
        "dp",
    )

    own_square = [squares_one[:, slot * width : (slot + 1) * width] for slot in range(3)] + [
        square_out,
        squares_two[:, :hidden_padded],
        squares_two[:, hidden_padded:],
        square_down,
    ]
    (stat_sums,) = kernel(
        statistics_body,
        [((8, 128), F32)],
        squares_one,
        magnitude_one,
        square_out,
        magnitude_out,
        squares_two,
        magnitude_two,
        square_down,
        magnitude_down,
    )
    stat_sums = total_over(stat_sums, "mp")[:7, :2]
    columns_all = jnp.array([weight.shape[1] for weight in weights], F32)[:, None]
    means = stat_sums / columns_all
    statistics = jnp.concatenate([jnp.sqrt(means[:, :1]), means[:, 1:]], axis=1)

    def rows_of(values, slot):
        return values[slot * R : (slot + 1) * R]

    scales_at = (11 + slabs) * R
    right_ends = [
        rows_of(last, 3 + slot)
        + negative_ratio(last[scales_at + 3 + slot][None], magnitude, square)
        * rows_of(crossed, slot)
        for slot, magnitude, square in (
            (0, magnitude_out, square_out),
            (1, magnitude_down, square_down),
        )
    ]
    down_rows = jnp.concatenate([rows_of(last, 11 + slab) for slab in range(slabs)], axis=1)
    left_grads = [rows_of(last, slot).T for slot in range(3)] + [
        rows_of(last, 10).T,
        rows_of(last, 5).T,
        rows_of(last, 6).T,
        down_rows[:, :hidden].T,
    ]
    right_grads = [rows_of(last, 7 + slot) for slot in range(3)] + [
        right_ends[0],
        rows_of(broad, 0)[:, :hidden],
        rows_of(broad, 1)[:, :hidden],
        right_ends[1],
    ]
    scale_grads = [last[scales_at + slot] for slot in range(4)] + [
        broad[2 * R, :hidden],
        broad[2 * R + 1, :hidden],
        last[scales_at + 4],
    ]
    results = [layer_out, input_gradient]
    for member in range(7):
        results += [
            left_grads[member],
            right_grads[member],
            scale_grads[member] / jnp.sqrt(own_square[member][0, : widths[member]]),
        ]
    return tuple(results + [statistics])


def solution(mesh):
    grid = P("dp", "mp")
    rows = P("mp", None)
    placed = (grid, grid, P("dp", None), P("mp"), P("mp")) + (rows,) * 7 + (rows, P(), P()) * 7
    adapters = (rows, P(None, "mp"), P("mp")) * 7
    return jax.shard_map(
        on_device,
        mesh=mesh,
        in_specs=placed,
        out_specs=(grid, grid) + adapters + (P(),),
        check_vma=False,
    )
```

time: 2190 us -> 501 us (0.23)
  waiting for transfers between devices: 1560 us -> 149 us
  matrix products: 236 us -> 0 us
  blocking collectives: 227 us -> 0 us
  Pallas kernels: 0 us -> 154 us
  starting transfers between devices: 13.2 us -> 158 us
  local copies, waits for them, and re-layouts: 70 us -> 11 us
  other arithmetic: 52.8 us -> 18.6 us
  between operations: 25.9 us -> 2.2 us
    reduce_scatter x9 -> x0, waiting for transfers between devices: 848 us -> none  [the longest x2 587 us: project_in(): lax.psum_scatter(partial_term(jnp.int32(0), members * column_count * lax....]
    psum x7 -> x0, waiting for transfers between devices: 317 us -> none  [the longest x5 229 us: rank_total(): return lax.psum(values, 'mp')]
    all_gather x4 -> x0, waiting for transfers between devices: 284 us -> none  [the longest x2 259 us: project_in_back(): return gradient_adder(kept, lax.all_gather(grads, 'mp', axis=1, tiled=True))]
    dot_general x85 -> x0, matrix products: 236 us -> none  [the longest x21 49.2 us: precise_cols(): lax.dot_general(left_part, right_part, (((1,), (1,)), ((), ())), precisio...]
    ppermute x0 -> x100, starting transfers between devices: none -> 158 us  [swap(): lax.ppermute(values, axis, [(place, place ^ offset) for place in range(co...]
    pallas_call x0 -> x35, Pallas kernels: none -> 154 us  [the longest x31 116 us: kernel(): pl.pallas_call(body, out_shape=tuple((jax.ShapeDtypeStruct(shape, kind) f...]
    ppermute x0 -> x100, waiting for transfers between devices: none -> 149 us  [swap(): lax.ppermute(values, axis, [(place, place ^ offset) for place in range(co...]
    psum x5 -> x0, blocking collectives: 137 us -> none  [the longest x2 72.5 us: rank_total(): return lax.psum(values, 'mp')]
  transfers between devices with their start and end apart: 22 -> 100, of which waited for: 20 -> 36; matrix products, arithmetic and copies ran while one was open for 12% -> 3% of each run, Pallas kernels for 0% -> 26%
where the time goes in v1:
time: 501 us; the launch traced here: 492 us
  starting transfers between devices  158 us (32%)
  Pallas kernels  154 us (31%)
  waiting for transfers between devices  149 us (30%)
  other arithmetic  18.6 us (4%)
  local copies, waits for them, and re-layouts  11 us (2%)
    ppermute x100, starting transfers between devices, swap(): lax.ppermute(values, axis, [(place, place ^ offset) for place in range(co...  158 us
    ppermute x100, waiting for transfers between devices, swap(): lax.ppermute(values, axis, [(place, place ^ offset) for place in range(co...  149 us
    pallas_call x31, Pallas kernels, kernel(): pl.pallas_call(body, out_shape=tuple((jax.ShapeDtypeStruct(shape, kind) f...  116 us
    pallas_call x2, Pallas kernels, assemble(): pl.pallas_call(body if keep else body_alone, scratch_shapes=[] if keep el...  18.9 us
    pallas_call x2, Pallas kernels, by_rows(): pl.pallas_call(body, grid=(steps,), in_specs=[spec(operand.shape, slot <...  18.5 us
  transfers between devices with their start and end apart: 100, of which 36 were waited for; matrix products, arithmetic and copies ran while one was open for 3% of the time, Pallas kernels for 26%

profile of v1, /device:TPU:0, one launch (start us, length us, event | category | flops | bytes accessed | tf_op | source)
XLA Modules:
  0.0 492.5 jit_solution(544884593122516909)
XLA Ops:
  4.0 6.2 %shard_map.515 = (bf16[768,2048]{1,0:T(8,128)(2,1)}, bf16[16,2048]{1,0:T(8,128)(2,1)}, f32[1,2048]{1,0:T(1,128)}, f32[1,2048]{1,0:T(1,128)}, bf16[4,16,256]{2,1,0:T(8,128)(2,1)}, /*index=5*/bf16[4,16,256]{2,1,0:T(8,128)(2,1)}) custom-call(s32[2]{0:T(128)} %pad_add_fusion.place_ref.refs_0_, bf16[704,2048]{1,0:T(8,128)(2,1)} %weight_ref.3, ...), custom_call_target="tpu_custom_call" | custom-call | tf_op jit(solution)/shard_map/pallas_call | solution.py:113
  29.7 5.2 %shard_map.517 = (bf16[256,1536]{1,0:T(8,128)(2,1)}, bf16[64,1536]{1,0:T(8,128)(2,1)}, bf16[64,1536]{1,0:T(8,128)(2,1)}, bf16[64,1536]{1,0:T(8,128)(2,1)}, bf16[...) custom-call(s32[2]{0:T(128)} %pad_add_fusion.place_ref.refs_0_, ...), custom_call_target="tpu_custom_call" | custom-call | tf_op jit(solution)/shard_map/pallas_call | solution.py:113
  56.0 10.9 %collective-permute-done.44.refs_3_ = bf16[64,1536]{1,0:T(8,128)(2,1)S(1)} collective-permute-done((bf16[64,1536]{1,0:T(8,128)(2,1)}, bf16[64,1536]{1,0:T(8,128)(2,1)S(1)}, u32[]{:S(2)}, u32[]{:S(2)}) %collective-permute-start.44) | collective-permute-done | bytes 196640 | tf_op jit(solution)/shard_map/ppermute | solution.py:23
  67.0 5.0 %collective-permute-done.45.refs_4_ = bf16[64,1536]{1,0:T(8,128)(2,1)S(1)} collective-permute-done((bf16[64,1536]{1,0:T(8,128)(2,1)}, bf16[64,1536]{1,0:T(8,128)(2,1)S(1)}, u32[]{:S(2)}, u32[]{:S(2)}) %collective-permute-start.45) | collective-permute-done | bytes 196640 | tf_op jit(solution)/shard_map/ppermute | solution.py:23
  71.9 11.5 %collective-permute-start.47 = (bf16[64,1536]{1,0:T(8,128)(2,1)S(1)}, bf16[64,1536]{1,0:T(8,128)(2,1)S(1)}, u32[]{:S(2)}, u32[]{:S(2)}) collective-permute-start(bf16[64,1536]{1,0:T(8,128)(2,1)S(1)} %copy-done.97), channel_id=1, source_target_pairs={{0,7},{1,6},{2,5},{3,4},{4,3},{5,2},{6,1},{7,0},{8,15},{9,14},{10,... | collective-permute-start | bytes 589832 | tf_op jit(solution)/shard_map/ppermute | solution.py:23
  107.7 4.4 collective-permute-done.2.refs_3_
  118.6 15.3 %collective-permute-start.35 = (bf16[576,256]{1,0:T(8,128)(2,1)}, bf16[576,256]{1,0:T(8,128)(2,1)}, u32[]{:S(2)}, u32[]{:S(2)}) collective-permute-start(bf16[576,256]{1,0:T(8,128)(2,1)} %pad_maximum_fusion.refs_0_), channel_id=1, source_target_pairs={{0,2},{1,3},{2,0},{3,1},{4,6},{5,7},{6,4},{7,5},{8,10},{9,11},{10,... | collective-permute-start | bytes 884744 | tf_op jit(solution)/shard_map/ppermute | solution.py:23
  134.6 4.3 collective-permute-start.37
  141.4 8.6 %shard_map.509 = (bf16[2048,768]{1,0:T(8,128)(2,1)}, bf16[2048,768]{1,0:T(8,128)(2,1)}, f32[1,768]{1,0:T(1,128)}) custom-call(s32[2]{0:T(128)} %pad_add_fusion.place_ref.refs_0_, bf16[256,768]{1,0:T(8,128)(2,1)} %get-tuple-element.133.own_ref, bf16[96,2048]{1,0:T(8,128)(2,1)} %get-tuple-element.134.left_ref.refs_11_.refs_7_, ...), custom_call_target="tpu_custom_call" | custom-call | tf_op jit(solution)/shard_map/pallas_call | solution.py:329
  150.0 13.6 %shard_map.511 = (bf16[512,2048]{1,0:T(8,128)(2,1)}, f32[512,768]{1,0:T(8,128)}, f32[512,48]{1,0:T(8,128)}, bf16[512,256]{1,0:T(8,128)(2,1)}, bf16[512,256]{1,0:...) custom-call(bf16[624,256]{1,0:T(8,128)(2,1)} %copy-done.1, ...), custom_call_target="tpu_custom_call" | custom-call | tf_op jit(solution)/shard_map/pallas_call | solution.py:113
  164.0 4.6 collective-permute-done.26
  174.5 4.1 collective-permute-done.20.refs_1_
  179.8 4.5 collective-permute-done.18.refs_1_
  194.7 6.9 %collective-permute-done.23.refs_4_ = bf16[512,256]{1,0:T(8,128)(2,1)S(1)} collective-permute-done((bf16[512,256]{1,0:T(8,128)(2,1)}, bf16[512,256]{1,0:T(8,128)(2,1)S(1)}, u32[]{:S(2)}, u32[]{:S(2)}) %collective-permute-start.23) | collective-permute-done | bytes 262176 | tf_op jit(solution)/shard_map/ppermute | solution.py:23
  202.7 11.8 %collective-permute-done.21.refs_3_ = bf16[512,256]{1,0:T(8,128)(2,1)S(1)} collective-permute-done((bf16[512,256]{1,0:T(8,128)(2,1)}, bf16[512,256]{1,0:T(8,128)(2,1)S(1)}, u32[]{:S(2)}, u32[]{:S(2)}) %collective-permute-start.21) | collective-permute-done | bytes 262176 | tf_op jit(solution)/shard_map/ppermute | solution.py:23
  232.8 11.3 %collective-permute-done.30.refs_4_ = bf16[512,256]{1,0:T(8,128)(2,1)} collective-permute-done((bf16[512,256]{1,0:T(8,128)(2,1)}, bf16[512,256]{1,0:T(8,128)(2,1)}, u32[]{:S(2)}, u32[]{:S(2)}) %collective-permute-start.30) | collective-permute-done | bytes 262176 | tf_op jit(solution)/shard_map/ppermute | solution.py:23
  246.8 5.7 %shard_map.518 = (bf16[64,2048]{1,0:T(8,128)(2,1)}, bf16[512,2048]{1,0:T(8,128)(2,1)}, f32[512,768]{1,0:T(8,128)}) custom-call(bf16[576,256]{1,0:T(8,128)(2,1)} %pad_maximum_fusion.refs_0_, bf16[576,256]{1,0:T(8,128)(2,1)} %collective-permute-done.34.refs_1_, bf16[576,256]{1,0:T(8,128)(2,1)} %collective-permute-done.35.refs_2_, bf16[576,256]{1,0:T(8,128)(2,1)} %copy-done.16, ...), custom_call_target="tpu_custom_call" | custom-call | tf_op jit(solution)/shard_map/pallas_call | solution.py:113
  252.5 10.3 %shard_map.520 = (bf16[2048,1536]{1,0:T(8,128)(2,1)}, f32[1,1536]{1,0:T(1,128)}) custom-call(s32[2]{0:T(128)} %pad_add_fusion.place_ref.refs_0_, bf16[256,1536]{1,0:T(8,128)(2,1)} %get-tuple-element.160.refs_1_, bf16[64,2048]{1,0:T(8,128)(2,1)} %get-tuple-element.163.refs_2_.left_ref, bf16[64,1536]{1,0:T(8,128)(2,1)} %get-tuple-element.164.refs_3_.right_ref, ...), custom_call_target="tpu_custom_call" | custom-call | tf_op jit(solution)/shard_map/pallas_call | solution.py:329
  263.8 13.5 %shard_map.521 = (bf16[512,2048]{1,0:T(8,128)(2,1)}, f32[512,1]{1,0:T(8,128)}, bf16[512,768]{1,0:T(8,128)(2,1)}, bf16[512,1536]{1,0:T(8,128)(2,1)}, f32[1,1536]{...) custom-call(bf16[512,256]{1,0:T(8,128)(2,1)} %get-tuple-element.158., ...), custom_call_target="tpu_custom_call" | custom-call | tf_op jit(solution)/shard_map/pallas_call | solution.py:130
  281.4 5.0 %shard_map.522 = (bf16[512,256]{1,0:T(8,128)(2,1)}, bf16[512,256]{1,0:T(8,128)(2,1)}, bf16[512,256]{1,0:T(8,128)(2,1)}, bf16[512,256]{1,0:T(8,128)(2,1)}, bf16[5...) custom-call(bf16[512,768]{1,0:T(8,128)(2,1)} %get-tuple-element.176.act_ref., ...), custom_call_target="tpu_custom_call" | custom-call | tf_op jit(solution)/shard_map/pallas_call | solution.py:130
  290.7 5.0 %collective-permute-done.97 = f32[8,128]{1,0:T(8,128)S(1)} collective-permute-done((f32[8,128]{1,0:T(8,128)}, f32[8,128]{1,0:T(8,128)S(1)}, u32[]{:S(2)}, u32[]{:S(2)}) %collective-permute-start.97) | collective-permute-done | bytes 4128 | tf_op jit(solution)/shard_map/ppermute | solution.py:23
  295.6 8.3 %collective-permute-start.66 = (f32[1,512]{1,0:T(1,128)S(1)}, f32[1,512]{1,0:T(1,128)S(1)}, u32[]{:S(2)}, u32[]{:S(2)}) collective-permute-start(f32[1,512]{1,0:T(1,128)S(1)} %add.75), channel_id=1, source_target_pairs={{0,2},{1,3},{2,0},{3,1},{4,6},{5,7},{6,4},{7,5},{8,10},{9,11},{10,... | collective-permute-start | bytes 6152 | tf_op jit(solution)/shard_map/ppermute | solution.py:23
  326.6 5.0 %collective-permute-done.98 = f32[8,128]{1,0:T(8,128)S(1)} collective-permute-done((f32[8,128]{1,0:T(8,128)S(1)}, f32[8,128]{1,0:T(8,128)S(1)}, u32[]{:S(2)}, u32[]{:S(2)}) %collective-permute-start.98) | collective-permute-done | bytes 4128 | tf_op jit(solution)/shard_map/ppermute | solution.py:23
  336.5 11.3 %collective-permute-done.62.refs_3_ = bf16[512,256]{1,0:T(8,128)(2,1)S(1)} collective-permute-done((bf16[512,256]{1,0:T(8,128)(2,1)}, bf16[512,256]{1,0:T(8,128)(2,1)S(1)}, u32[]{:S(2)}, u32[]{:S(2)}) %collective-permute-start.62) | collective-permute-done | bytes 262176 | tf_op jit(solution)/shard_map/ppermute | solution.py:23
  367.6 9.7 %shard_map.536 = (f32[40,768]{1,0:T(8,128)}, bf16[4,32,256]{2,1,0:T(8,128)(2,1)}, bf16[4,32,256]{2,1,0:T(8,128)(2,1)}) custom-call(bf16[512,1536]{1,0:T(8,128)(2,1)} %get-tuple-element.227.low_ref, bf16[512,2048]{1,0:T(8,128)(2,1)} %get-tuple-element.228.scaled_ref, f32[512,1]{1,0:T(8,128)} %get-tuple-element.196.refs_7_.inverse_ref, ...), custom_call_target="tpu_custom_call" | custom-call | tf_op jit(solution)/shard_map/pallas_call | solution.py:113
  385.8 7.3 %collective-permute-done.69.refs_2_ = bf16[512,256]{1,0:T(8,128)(2,1)S(1)} collective-permute-done((bf16[512,256]{1,0:T(8,128)(2,1)S(1)}, bf16[512,256]{1,0:T(8,128)(2,1)S(1)}, u32[]{:S(2)}, u32[]{:S(2)}) %collective-permute-start.69) | collective-permute-done | bytes 262176 | tf_op jit(solution)/shard_map/ppermute | solution.py:23
  394.2 7.5 %collective-permute-done.71.refs_4_ = bf16[512,256]{1,0:T(8,128)(2,1)S(1)} collective-permute-done((bf16[512,256]{1,0:T(8,128)(2,1)S(1)}, bf16[512,256]{1,0:T(8,128)(2,1)S(1)}, u32[]{:S(2)}, u32[]{:S(2)}) %collective-permute-start.71) | collective-permute-done | bytes 262176 | tf_op jit(solution)/shard_map/ppermute | solution.py:23
  403.8 5.1 %collective-permute-done.72.refs_5_ = bf16[512,256]{1,0:T(8,128)(2,1)S(1)} collective-permute-done((bf16[512,256]{1,0:T(8,128)(2,1)S(1)}, bf16[512,256]{1,0:T(8,128)(2,1)S(1)}, u32[]{:S(2)}, u32[]{:S(2)}) %collective-permute-start.72) | collective-permute-done | bytes 262176 | tf_op jit(solution)/shard_map/ppermute | solution.py:23
  412.4 9.9 %shard_map.531 = (bf16[512,2048]{1,0:T(8,128)(2,1)}, bf16[512,768]{1,0:T(8,128)(2,1)}, f32[1,768]{1,0:T(1,128)}, f32[1,512]{1,0:T(1,128)}, bf16[512,256]{1,0:T(8...) custom-call(bf16[512,256]{1,0:T(8,128)(2,1)} %get-tuple-element.199., ...), custom_call_target="tpu_custom_call" | custom-call | tf_op jit(solution)/shard_map/pallas_call | solution.py:113
  422.3 11.8 %shard_map.537 = (f32[120,256]{1,0:T(8,128)}, bf16[4,144,256]{2,1,0:T(8,128)(2,1)}, bf16[4,144,256]{2,1,0:T(8,128)(2,1)}) custom-call(bf16[512,768]{1,0:T(8,128)(2,1)} %get-tuple-element.218.refs_0_, bf16[512,2048]{1,0:T(8,128)(2,1)} %get-tuple-element.219.refs_1_, f32[512,48]{1,0:T(8,128)} %get-tuple-element.220.refs_2_, ...), custom_call_target="tpu_custom_call" | custom-call | tf_op jit(solution)/shard_map/pallas_call | solution.py:113
  435.7 4.1 shard_map.538
  474.0 11.4 %collective-permute-done.79.refs_3_ = bf16[512,256]{1,0:T(8,128)(2,1)S(1)} collective-permute-done((bf16[512,256]{1,0:T(8,128)(2,1)}, bf16[512,256]{1,0:T(8,128)(2,1)S(1)}, u32[]{:S(2)}, u32[]{:S(2)}) %collective-permute-start.79) | collective-permute-done | bytes 262176 | tf_op jit(solution)/shard_map/ppermute | solution.py:23
  (496 shorter events, 231.2 us)
Async XLA Ops:
  15.0 20.2 %collective-permute-start.24 = (f32[8,2,256]{2,0,1:T(8,128)S(1)}, f32[8,2,256]{2,0,1:T(8,128)S(1)}, u32[]{:S(2)}, u32[]{:S(2)}) collective-permute-start(f32[8,2,256]{2,0,1:T(8,128)S(1)} %stack.38), channel_id=1, source_target_pairs={{0,1},{1,0},{2,3},{3,2},{4,5},{5,4},{6,7},{7,6},{8,9},{9,8},{10,11... | collective-permute-start | bytes 49160 | tf_op jit(solution)/shard_map/ppermute | solution.py:23
  45.1 21.9 %collective-permute-start.44 = (bf16[64,1536]{1,0:T(8,128)(2,1)}, bf16[64,1536]{1,0:T(8,128)(2,1)S(1)}, u32[]{:S(2)}, u32[]{:S(2)}) collective-permute-start(bf16[64,1536]{1,0:T(8,128)(2,1)} %get-tuple-element.168), channel_id=1, source_target_pairs={{0,4},{1,5},{2,6},{3,7},{4,0},{5,1},{6,2},{7,3},{8,12},{9,13},{10,... | collective-permute-start | bytes 589832 | tf_op jit(solution)/shard_map/ppermute | solution.py:23
  48.5 23.4 %collective-permute-start.45 = (bf16[64,1536]{1,0:T(8,128)(2,1)}, bf16[64,1536]{1,0:T(8,128)(2,1)S(1)}, u32[]{:S(2)}, u32[]{:S(2)}) collective-permute-start(bf16[64,1536]{1,0:T(8,128)(2,1)} %get-tuple-element.169), channel_id=1, source_target_pairs={{0,5},{1,4},{2,7},{3,6},{4,1},{5,0},{6,3},{7,2},{8,13},{9,12},{10,... | collective-permute-start | bytes 589832 | tf_op jit(solution)/shard_map/ppermute | solution.py:23
  53.5 30.0 %collective-permute-start.46 = (bf16[64,1536]{1,0:T(8,128)(2,1)}, bf16[64,1536]{1,0:T(8,128)(2,1)S(1)}, u32[]{:S(2)}, u32[]{:S(2)}) collective-permute-start(bf16[64,1536]{1,0:T(8,128)(2,1)} %get-tuple-element.170), channel_id=1, source_target_pairs={{0,6},{1,7},{2,4},{3,5},{4,2},{5,3},{6,0},{7,1},{8,14},{9,15},{10,... | collective-permute-start | bytes 589832 | tf_op jit(solution)/shard_map/ppermute | solution.py:23
  54.5 46.8 %collective-permute-start.15 = (bf16[7,64,768]{2,1,0:T(8,128)(2,1)}, bf16[7,64,768]{2,1,0:T(8,128)(2,1)}, u32[]{:S(2)}, u32[]{:S(2)}) collective-permute-start(bf16[7,64,768]{2,1,0:T(8,128)(2,1)} %shard_map.508.refs_0_), channel_id=1, source_target_pairs={{0,16},{8,24},{16,0},{24,8},{1,17},{9,25},{17,1},{25,9},{2,18},{10... | collective-permute-start | bytes 2064392 | tf_op jit(solution)/shard_map/ppermute | solution.py:23
  56.0 40.5 %collective-permute-start.1 = (bf16[624,256]{1,0:T(8,128)(2,1)S(1)}, bf16[624,256]{1,0:T(8,128)(2,1)S(1)}, u32[]{:S(2)}, u32[]{:S(2)}) collective-permute-start(bf16[624,256]{1,0:T(8,128)(2,1)S(1)} %concatenate.57.refs_0_), channel_id=1, source_target_pairs={{0,2},{1,3},{2,0},{3,1},{4,6},{5,7},{6,4},{7,5},{8,10},{9,11},{10,... | collective-permute-start | bytes 958472 | tf_op jit(solution)/shard_map/ppermute | solution.py:23
  67.0 33.1 %collective-permute-start.3 = (bf16[624,256]{1,0:T(8,128)(2,1)S(1)}, bf16[624,256]{1,0:T(8,128)(2,1)S(1)}, u32[]{:S(2)}, u32[]{:S(2)}) collective-permute-start(bf16[624,256]{1,0:T(8,128)(2,1)S(1)} %concatenate.57.refs_0_), channel_id=1, source_target_pairs={{0,4},{1,5},{2,6},{3,7},{4,0},{5,1},{6,2},{7,3},{8,12},{9,13},{10,... | collective-permute-start | bytes 958472 | tf_op jit(solution)/shard_map/ppermute | solution.py:23
  94.9 75.8 %collective-permute-start.49 = (bf16[7,64,1536]{2,1,0:T(8,128)(2,1)}, bf16[7,64,1536]{2,1,0:T(8,128)(2,1)S(1)}, u32[]{:S(2)}, u32[]{:S(2)}) collective-permute-start(bf16[7,64,1536]{2,1,0:T(8,128)(2,1)} %shard_map.519.refs_4_), channel_id=1, source_target_pairs={{0,16},{8,24},{16,0},{24,8},{1,17},{9,25},{17,1},{25,9},{2,18},{10... | collective-permute-start | bytes 4128776 | tf_op jit(solution)/shard_map/ppermute | solution.py:23
  101.2 40.2 %collective-permute-start.14 = (bf16[7,64,768]{2,1,0:T(8,128)(2,1)S(1)}, bf16[7,64,768]{2,1,0:T(8,128)(2,1)}, u32[]{:S(2)}, u32[]{:S(2)}) collective-permute-start(bf16[7,64,768]{2,1,0:T(8,128)(2,1)S(1)} %copy-done.2), channel_id=1, source_target_pairs={{0,8},{8,0},{16,24},{24,16},{1,9},{9,1},{17,25},{25,17},{2,10},{10... | collective-permute-start | bytes 2064392 | tf_op jit(solution)/shard_map/ppermute | solution.py:23
  101.2 40.1 %collective-permute-start.16 = (bf16[7,64,768]{2,1,0:T(8,128)(2,1)}, bf16[7,64,768]{2,1,0:T(8,128)(2,1)}, u32[]{:S(2)}, u32[]{:S(2)}) collective-permute-start(bf16[7,64,768]{2,1,0:T(8,128)(2,1)} %collective-permute-done.15.refs_2_), channel_id=1, source_target_pairs={{0,8},{8,0},{16,24},{24,16},{1,9},{9,1},{17,25},{25,17},{2,10},{10... | collective-permute-start | bytes 2064392 | tf_op jit(solution)/shard_map/ppermute | solution.py:23
  112.1 21.8 %collective-permute-start.6 = (bf16[624,256]{1,0:T(8,128)(2,1)S(1)}, bf16[624,256]{1,0:T(8,128)(2,1)S(1)}, u32[]{:S(2)}, u32[]{:S(2)}) collective-permute-start(bf16[624,256]{1,0:T(8,128)(2,1)S(1)} %collective-permute-done.5.refs_6_), channel_id=1, source_target_pairs={{0,1},{1,0},{2,3},{3,2},{4,5},{5,4},{6,7},{7,6},{8,9},{9,8},{10,11... | collective-permute-start | bytes 958472 | tf_op jit(solution)/shard_map/ppermute | solution.py:23
  118.6 51.8 %collective-permute-start.35 = (bf16[576,256]{1,0:T(8,128)(2,1)}, bf16[576,256]{1,0:T(8,128)(2,1)}, u32[]{:S(2)}, u32[]{:S(2)}) collective-permute-start(bf16[576,256]{1,0:T(8,128)(2,1)} %pad_maximum_fusion.refs_0_), channel_id=1, source_target_pairs={{0,2},{1,3},{2,0},{3,1},{4,6},{5,7},{6,4},{7,5},{8,10},{9,11},{10,... | collective-permute-start | bytes 884744 | tf_op jit(solution)/shard_map/ppermute | solution.py:23
  134.6 36.1 %collective-permute-start.37 = (bf16[576,256]{1,0:T(8,128)(2,1)}, bf16[576,256]{1,0:T(8,128)(2,1)}, u32[]{:S(2)}, u32[]{:S(2)}) collective-permute-start(bf16[576,256]{1,0:T(8,128)(2,1)} %pad_maximum_fusion.refs_0_), channel_id=1, source_target_pairs={{0,4},{1,5},{2,6},{3,7},{4,0},{5,1},{6,2},{7,3},{8,12},{9,13},{10,... | collective-permute-start | bytes 884744 | tf_op jit(solution)/shard_map/ppermute | solution.py:23
  170.7 60.1 %collective-permute-start.48 = (bf16[7,64,1536]{2,1,0:T(8,128)(2,1)S(1)}, bf16[7,64,1536]{2,1,0:T(8,128)(2,1)}, u32[]{:S(2)}, u32[]{:S(2)}) collective-permute-start(bf16[7,64,1536]{2,1,0:T(8,128)(2,1)S(1)} %copy-done), channel_id=1, source_target_pairs={{0,8},{8,0},{16,24},{24,16},{1,9},{9,1},{17,25},{25,17},{2,10},{10... | collective-permute-start | bytes 4128776 | tf_op jit(solution)/shard_map/ppermute | solution.py:23
  184.3 68.3 %collective-permute-start.50 = (bf16[7,64,1536]{2,1,0:T(8,128)(2,1)S(1)}, bf16[7,64,1536]{2,1,0:T(8,128)(2,1)}, u32[]{:S(2)}, u32[]{:S(2)}) collective-permute-start(bf16[7,64,1536]{2,1,0:T(8,128)(2,1)S(1)} %collective-permute-done.49.refs_6_), channel_id=1, source_target_pairs={{0,8},{8,0},{16,24},{24,16},{1,9},{9,1},{17,25},{25,17},{2,10},{10... | collective-permute-start | bytes 4128776 | tf_op jit(solution)/shard_map/ppermute | solution.py:23
  192.3 22.2 %collective-permute-start.21 = (bf16[512,256]{1,0:T(8,128)(2,1)}, bf16[512,256]{1,0:T(8,128)(2,1)S(1)}, u32[]{:S(2)}, u32[]{:S(2)}) collective-permute-start(bf16[512,256]{1,0:T(8,128)(2,1)} %shard_map.513), channel_id=1, source_target_pairs={{0,4},{1,5},{2,6},{3,7},{4,0},{5,1},{6,2},{7,3},{8,12},{9,13},{10,... | collective-permute-start | bytes 786440 | tf_op jit(solution)/shard_map/ppermute | solution.py:23
  193.3 22.4 %collective-permute-start.19 = (bf16[512,256]{1,0:T(8,128)(2,1)}, bf16[512,256]{1,0:T(8,128)(2,1)S(1)}, u32[]{:S(2)}, u32[]{:S(2)}) collective-permute-start(bf16[512,256]{1,0:T(8,128)(2,1)} %shard_map.512), channel_id=1, source_target_pairs={{0,2},{1,3},{2,0},{3,1},{4,6},{5,7},{6,4},{7,5},{8,10},{9,11},{10,... | collective-permute-start | bytes 786440 | tf_op jit(solution)/shard_map/ppermute | solution.py:23
  230.8 32.0 %collective-permute-start.27 = (bf16[512,256]{1,0:T(8,128)(2,1)}, bf16[512,256]{1,0:T(8,128)(2,1)S(1)}, u32[]{:S(2)}, u32[]{:S(2)}) collective-permute-start(bf16[512,256]{1,0:T(8,128)(2,1)} %get-tuple-element.158.refs_0_), channel_id=1, source_target_pairs={{0,1},{1,0},{2,3},{3,2},{4,5},{5,4},{6,7},{7,6},{8,9},{9,8},{10,11... | collective-permute-start | bytes 786440 | tf_op jit(solution)/shard_map/ppermute | solution.py:23
  232.0 30.8 %collective-permute-start.29 = (bf16[512,256]{1,0:T(8,128)(2,1)}, bf16[512,256]{1,0:T(8,128)(2,1)S(1)}, u32[]{:S(2)}, u32[]{:S(2)}) collective-permute-start(bf16[512,256]{1,0:T(8,128)(2,1)} %collective-permute-done.28.refs_2_), channel_id=1, source_target_pairs={{0,1},{1,0},{2,3},{3,2},{4,5},{5,4},{6,7},{7,6},{8,9},{9,8},{10,11... | collective-permute-start | bytes 786440 | tf_op jit(solution)/shard_map/ppermute | solution.py:23
  278.3 28.2 %collective-permute-start.63 = (bf16[512,256]{1,0:T(8,128)(2,1)}, bf16[512,256]{1,0:T(8,128)(2,1)S(1)}, u32[]{:S(2)}, u32[]{:S(2)}) collective-permute-start(bf16[512,256]{1,0:T(8,128)(2,1)} %get-tuple-element.195), channel_id=1, source_target_pairs={{0,1},{1,0},{2,3},{3,2},{4,5},{5,4},{6,7},{7,6},{8,9},{9,8},{10,11... | collective-permute-start | bytes 786440 | tf_op jit(solution)/shard_map/ppermute | solution.py:23
  279.4 28.1 %collective-permute-start.61 = (bf16[512,256]{1,0:T(8,128)(2,1)}, bf16[512,256]{1,0:T(8,128)(2,1)S(1)}, u32[]{:S(2)}, u32[]{:S(2)}) collective-permute-start(bf16[512,256]{1,0:T(8,128)(2,1)} %get-tuple-element.193), channel_id=1, source_target_pairs={{0,1},{1,0},{2,3},{3,2},{4,5},{5,4},{6,7},{7,6},{8,9},{9,8},{10,11... | collective-permute-start | bytes 786440 | tf_op jit(solution)/shard_map/ppermute | solution.py:23
  280.4 34.5 %collective-permute-start.59 = (bf16[512,256]{1,0:T(8,128)(2,1)}, bf16[512,256]{1,0:T(8,128)(2,1)S(1)}, u32[]{:S(2)}, u32[]{:S(2)}) collective-permute-start(bf16[512,256]{1,0:T(8,128)(2,1)} %get-tuple-element.191), channel_id=1, source_target_pairs={{0,1},{1,0},{2,3},{3,2},{4,5},{5,4},{6,7},{7,6},{8,9},{9,8},{10,11... | collective-permute-start | bytes 786440 | tf_op jit(solution)/shard_map/ppermute | solution.py:23
  286.4 30.2 %collective-permute-start.56 = (bf16[512,256]{1,0:T(8,128)(2,1)}, bf16[512,256]{1,0:T(8,128)(2,1)S(1)}, u32[]{:S(2)}, u32[]{:S(2)}) collective-permute-start(bf16[512,256]{1,0:T(8,128)(2,1)} %get-tuple-element.184), channel_id=1, source_target_pairs={{0,1},{1,0},{2,3},{3,2},{4,5},{5,4},{6,7},{7,6},{8,9},{9,8},{10,11... | collective-permute-start | bytes 786440 | tf_op jit(solution)/shard_map/ppermute | solution.py:23
  314.8 20.4 %collective-permute-start.64 = (bf16[512,256]{1,0:T(8,128)(2,1)}, bf16[512,256]{1,0:T(8,128)(2,1)S(1)}, u32[]{:S(2)}, u32[]{:S(2)}) collective-permute-start(bf16[512,256]{1,0:T(8,128)(2,1)} %shard_map.529), channel_id=1, source_target_pairs={{0,6},{1,7},{2,4},{3,5},{4,2},{5,3},{6,0},{7,1},{8,14},{9,15},{10,... | collective-permute-start | bytes 786440 | tf_op jit(solution)/shard_map/ppermute | solution.py:23
  316.7 31.1 %collective-permute-start.62 = (bf16[512,256]{1,0:T(8,128)(2,1)}, bf16[512,256]{1,0:T(8,128)(2,1)S(1)}, u32[]{:S(2)}, u32[]{:S(2)}) collective-permute-start(bf16[512,256]{1,0:T(8,128)(2,1)} %shard_map.528), channel_id=1, source_target_pairs={{0,4},{1,5},{2,6},{3,7},{4,0},{5,1},{6,2},{7,3},{8,12},{9,13},{10,... | collective-permute-start | bytes 786440 | tf_op jit(solution)/shard_map/ppermute | solution.py:23
  318.6 29.9 %collective-permute-start.60 = (bf16[512,256]{1,0:T(8,128)(2,1)}, bf16[512,256]{1,0:T(8,128)(2,1)S(1)}, u32[]{:S(2)}, u32[]{:S(2)}) collective-permute-start(bf16[512,256]{1,0:T(8,128)(2,1)} %shard_map.527), channel_id=1, source_target_pairs={{0,2},{1,3},{2,0},{3,1},{4,6},{5,7},{6,4},{7,5},{8,10},{9,11},{10,... | collective-permute-start | bytes 786440 | tf_op jit(solution)/shard_map/ppermute | solution.py:23
  331.6 23.5 %collective-permute-start.51 = (bf16[512,256]{1,0:T(8,128)(2,1)S(1)}, bf16[512,256]{1,0:T(8,128)(2,1)S(1)}, u32[]{:S(2)}, u32[]{:S(2)}) collective-permute-start(bf16[512,256]{1,0:T(8,128)(2,1)S(1)} %copy-done.95), channel_id=1, source_target_pairs={{0,1},{1,0},{2,3},{3,2},{4,5},{5,4},{6,7},{7,6},{8,9},{9,8},{10,11... | collective-permute-start | bytes 786440 | tf_op jit(solution)/shard_map/ppermute | solution.py:23
  332.5 22.6 %collective-permute-start.57 = (bf16[512,256]{1,0:T(8,128)(2,1)}, bf16[512,256]{1,0:T(8,128)(2,1)S(1)}, u32[]{:S(2)}, u32[]{:S(2)}) collective-permute-start(bf16[512,256]{1,0:T(8,128)(2,1)} %shard_map.525), channel_id=1, source_target_pairs={{0,6},{1,7},{2,4},{3,5},{4,2},{5,3},{6,0},{7,1},{8,14},{9,15},{10,... | collective-permute-start | bytes 786440 | tf_op jit(solution)/shard_map/ppermute | solution.py:23
  335.2 21.6 %collective-permute-start.55 = (bf16[512,256]{1,0:T(8,128)(2,1)}, bf16[512,256]{1,0:T(8,128)(2,1)S(1)}, u32[]{:S(2)}, u32[]{:S(2)}) collective-permute-start(bf16[512,256]{1,0:T(8,128)(2,1)} %shard_map.524), channel_id=1, source_target_pairs={{0,4},{1,5},{2,6},{3,7},{4,0},{5,1},{6,2},{7,3},{8,12},{9,13},{10,... | collective-permute-start | bytes 786440 | tf_op jit(solution)/shard_map/ppermute | solution.py:23
  348.4 28.9 %collective-permute-start.99 = (f32[8,128]{1,0:T(8,128)S(1)}, f32[8,128]{1,0:T(8,128)S(1)}, u32[]{:S(2)}, u32[]{:S(2)}) collective-permute-start(f32[8,128]{1,0:T(8,128)S(1)} %add.93), channel_id=1, source_target_pairs={{0,4},{1,5},{2,6},{3,7},{4,0},{5,1},{6,2},{7,3},{8,12},{9,13},{10,... | collective-permute-start | bytes 12296 | tf_op jit(solution)/shard_map/ppermute | solution.py:23
  379.8 74.8 %collective-permute-start.96 = (f32[40,768]{1,0:T(8,128)S(1)}, f32[40,768]{1,0:T(8,128)S(1)}, u32[]{:S(2)}, u32[]{:S(2)}) collective-permute-start(f32[40,768]{1,0:T(8,128)S(1)} %add.89), channel_id=1, source_target_pairs={{0,16},{8,24},{16,0},{24,8},{1,17},{9,25},{17,1},{25,9},{2,18},{10... | collective-permute-start | bytes 368648 | tf_op jit(solution)/shard_map/ppermute | solution.py:23
  380.4 21.3 %collective-permute-start.71 = (bf16[512,256]{1,0:T(8,128)(2,1)S(1)}, bf16[512,256]{1,0:T(8,128)(2,1)S(1)}, u32[]{:S(2)}, u32[]{:S(2)}) collective-permute-start(bf16[512,256]{1,0:T(8,128)(2,1)S(1)} %copy-done.17), channel_id=1, source_target_pairs={{0,4},{1,5},{2,6},{3,7},{4,0},{5,1},{6,2},{7,3},{8,12},{9,13},{10,... | collective-permute-start | bytes 786440 | tf_op jit(solution)/shard_map/ppermute | solution.py:23
  (171 other events, 2393.3 us)

commit v2 on v1

--- a/solution.py
+++ b/solution.py
@@ -44,14 +44,6 @@
     return values
 
 
-def small_gather(chunk):
-    count = lax.axis_size("mp")
-    inner = count // PLANES
-    held = jnp.stack([chunk] + [swap(chunk, a * inner, "mp") for a in range(1, PLANES)])
-    sides = [held] + [swap(held, b, "mp") for b in range(1, inner)]
-    return jnp.concatenate([sides[k % inner][k // inner] for k in range(count)], axis=1)
-
-
 def small_scatter(bundles):
     inner = len(bundles)
     held = bundles[0].astype(F32)
@@ -64,14 +56,15 @@
     return final
 
 
-def total_relative(values):
+def total_relative(values, same):
     count = values.shape[0]
     offset = 1
     while offset < count:
-        turned = jnp.stack([values[k ^ offset] for k in range(count)])
-        values = values + swap(turned, offset, "mp")
+        turned = [values[k ^ offset][None] for k in range(count)]
+        got = swap(jnp.concatenate(turned + [same]), offset, "mp")
+        values, same = values + got[:count], same + got[count:]
         offset *= 2
-    return values
+    return values, same
 
 
 def dot(left_part, right_part, left_dim=1, right_dim=0):
@@ -105,7 +98,7 @@
     return jnp.pad(values, widths)
 
 
-def kernel(body, outs, *operands, scalars=None):
+def kernel(body, outs, *operands, scalars=None, scratch=()):
     specs = [pl.BlockSpec(memory_space=pltpu.VMEM)] * len(operands)
     if scalars is not None:
         specs = [pl.BlockSpec(memory_space=pltpu.SMEM)] + specs
@@ -114,6 +107,7 @@
         body,
         out_shape=tuple(jax.ShapeDtypeStruct(shape, kind) for shape, kind in outs),
         in_specs=specs,
+        scratch_shapes=list(scratch),
     )(*operands)
 
 
@@ -233,14 +227,16 @@
     width = chunks[0].shape[1]
 
     def body(*refs):
-        left_ref, gain_ref = refs[-2:]
-        for k, ref in enumerate(refs[:-2]):
+        one_ref, two_ref, gain_ref = refs[-3:]
+        first, second = tokens + 6 * R, tokens + 8 * R
+        for k, ref in enumerate(refs[:-3]):
             lanes = slice(k * width, (k + 1) * width)
-            left_ref[:, lanes] = ref[tokens : tokens + 6 * R, :]
-            gain_ref[:, lanes] = ref[tokens + 6 * R : tokens + 6 * R + 16, :].astype(F32)[1:2]
+            one_ref[:, lanes] = ref[tokens:first, :]
+            two_ref[:, lanes] = ref[first:second, :]
+            gain_ref[:, lanes] = ref[second : second + 16, :].astype(F32)[1:2]
 
     total = len(chunks) * width
-    outs = [((6 * R, total), LOW), ((1, total), F32)]
+    outs = [((6 * R, total), LOW), ((2 * R, total), LOW), ((1, total), F32)]
     return kernel(body, outs, *chunks)
 
 
@@ -294,6 +290,12 @@
     return jnp.concatenate([high, high, rest] if swapped else [high, rest, high], axis=0)
 
 
+def fold_factors(lefts, rights_pair):
+    if lefts.shape[0] == rights_pair.shape[0]:
+        return thrice(lefts, False), thrice(rights_pair, True)
+    return jnp.concatenate([lefts, lefts], axis=0), rights_pair
+
+
 def assemble(own, pieces, lefts_all, rights_pair, scalars, keep):
     count = lax.axis_size("mp")
     rows, wide = own.shape
@@ -316,7 +318,7 @@
                 weight_ref[pl.ds(at, part), :] = ref[0]
 
         full = weight_ref[...].astype(F32) + dot(
-            thrice(left_ref[...], False), thrice(right_ref[...], True), 0, 0
+            *fold_factors(left_ref[...], right_ref[...]), 0, 0
         )
         full_ref[...] = full.astype(LOW)
         square_ref[...] += jnp.sum(full * full, axis=0, keepdims=True)
@@ -360,24 +362,30 @@
         moved_ref,
         *cross_refs,
     ):
+        inner = count // PLANES
         lefts = thrice(left_ref[...], False)
-        for k in range(count):
-            at = pl.ds(pl.multiple_of((place_ref[0] ^ k) * width, width), width)
-            lanes = slice(k * width, (k + 1) * width)
-            values = weight_ref[:, at]
-            if rows < rows_padded:
-                fill = jnp.zeros((rows_padded - rows, width), LOW)
-                values = jnp.concatenate([values, fill], axis=0)
-            high, rest = split(right_ref[:, at])
-            pair = jnp.concatenate([high, rest], axis=0)
-            high_ref[:, lanes] = high
-            moved_ref[:, lanes] = magnitude_ref[:, at]
-            full = values.astype(F32) + dot(lefts, thrice(pair, True), 0, 0)
-            low = full.astype(LOW)
-            full_ref[:, lanes] = low
-            square_ref[:, lanes] = jnp.sum(full * full, axis=0, keepdims=True)
-            a, b = divmod(k, count // PLANES)
-            cross_refs[b][a] = dot(left_ref[:R, :], low).astype(LOW)
+
+        def one_plane(a, carry):
+            for b in range(inner):
+                k = a * inner + b
+                at = pl.ds(pl.multiple_of((place_ref[0] ^ k) * width, width), width)
+                lanes = pl.ds(pl.multiple_of(k * width, width), width)
+                values = weight_ref[:, at]
+                if rows < rows_padded:
+                    fill = jnp.zeros((rows_padded - rows, width), LOW)
+                    values = jnp.concatenate([values, fill], axis=0)
+                high, rest = split(right_ref[:, at])
+                pair = jnp.concatenate([high, rest], axis=0)
+                high_ref[:, lanes] = high
+                moved_ref[:, lanes] = magnitude_ref[:, at]
+                full = values.astype(F32) + dot(lefts, thrice(pair, True), 0, 0)
+                low = full.astype(LOW)
+                full_ref[:, lanes] = low
+                square_ref[:, lanes] = jnp.sum(full * full, axis=0, keepdims=True)
+                cross_refs[b][a] = dot(left_ref[:R, :], low).astype(LOW)
+            return carry
+
+        lax.fori_loop(0, PLANES, one_plane, 0)
 
     return kernel(
         body,
@@ -396,11 +404,6 @@
     )
 
 
-def inner_product(inputs, lefts_pair):
-    half = lefts_pair.shape[0] // 2
-    return dot(inputs, lefts_pair[:half], 1, 1) + dot(inputs, lefts_pair[half:], 1, 1)
-
-
 def adapter_term(inner, rights_pair):
     half = rights_pair.shape[0] // 2
     high, rest = split(inner)
@@ -413,11 +416,17 @@
     return pltpu.roll(values, HD // 2, axis=1)
 
 
-def allowed_pairs(seg_rows, seg_cols):
-    length = seg_rows.shape[0]
-    row_at = lax.broadcasted_iota(jnp.int32, (length, length), 0)
-    col_at = lax.broadcasted_iota(jnp.int32, (length, length), 1)
-    return (seg_rows == seg_cols) & (col_at <= row_at)
+def query_blocks(tokens):
+    size = tokens // 2
+    return [(slice(at, at + size), slice(0, at + size)) for at in range(0, tokens, size)]
+
+
+def masked_logits(q_ref, k_ref, segr_ref, segc_ref, lanes, rows, seen):
+    logits = dot(q_ref[rows, lanes], k_ref[seen, lanes], 1, 1) * HD ** (-0.5)
+    row_at = rows.start + lax.broadcasted_iota(jnp.int32, logits.shape, 0)
+    col_at = lax.broadcasted_iota(jnp.int32, logits.shape, 1)
+    allowed = (segr_ref[rows, :] == segc_ref[:, seen]) & (col_at <= row_at)
+    return jnp.where(allowed, logits, NEGATIVE)
 
 
 def lane_sums_as_row(values):
@@ -478,32 +487,34 @@
         values = ref[:tokens, :].astype(F32)
         normed_ref[:, k * width : (k + 1) * width] = (values * inverse * gain).astype(LOW)
     normed = normed_ref[...]
-    inner = inner_product(normed, left_ref[...])
+    half = left_ref.shape[0] // 2
+    inner = dot(normed, left_ref[:half, :], 1, 1) + dot(normed, left_ref[half:, :], 1, 1)
     inner_ref[...] = inner
     proj_ref[...] = dot(normed, weight_ref[...]) + adapter_term(inner, right_ref[...])
     factor_ref[...] = magnitude_ref[...] / jnp.sqrt(square_ref[...])
     cosine = cos_ref[...]
     sine = sin_ref[...]
-    allowed = allowed_pairs(segr_ref[...], segc_ref[...])
-    for head in range(heads):
-        at = head * HD
-        taken = []
-        for member in range(3):
-            lanes = slice(member * width + at, member * width + at + HD)
-            taken.append(proj_ref[:, lanes] * factor_ref[:, lanes])
-        queries = (taken[0] * cosine + halves_turned(taken[0]) * sine).astype(LOW)
-        keys = (taken[1] * cosine + halves_turned(taken[1]) * sine).astype(LOW)
-        values = taken[2].astype(LOW)
-        logits = jnp.where(allowed, dot(queries, keys, 1, 1) * HD ** (-0.5), NEGATIVE)
-        highest = jnp.max(logits, axis=1, keepdims=True)
-        powers = jnp.exp(logits - highest)
-        totals = jnp.sum(powers, axis=1, keepdims=True)
-        probs_low = (powers / totals).astype(LOW)
-        mix_ref[:, at : at + HD] = dot(probs_low, values).astype(LOW)
-        q_ref[:, at : at + HD] = queries
-        k_ref[:, at : at + HD] = keys
-        v_ref[:, at : at + HD] = values
-        lse_ref[:, head : head + 1] = highest + jnp.log(totals)
+
+    def one_head(head, carry):
+        lanes = [
+            pl.ds(pl.multiple_of(member * width + head * HD, HD), HD) for member in range(3)
+        ]
+        taken = [proj_ref[:, at] * factor_ref[:, at] for at in lanes]
+        at = lanes[0]
+        q_ref[:, at] = (taken[0] * cosine + halves_turned(taken[0]) * sine).astype(LOW)
+        k_ref[:, at] = (taken[1] * cosine + halves_turned(taken[1]) * sine).astype(LOW)
+        v_ref[:, at] = taken[2].astype(LOW)
+        for rows, seen in query_blocks(tokens):
+            logits = masked_logits(q_ref, k_ref, segr_ref, segc_ref, at, rows, seen)
+            highest = jnp.max(logits, axis=1, keepdims=True)
+            powers = jnp.exp(logits - highest)
+            totals = jnp.sum(powers, axis=1, keepdims=True)
+            probs_low = (powers / totals).astype(LOW)
+            mix_ref[rows, at] = dot(probs_low, v_ref[seen, at]).astype(LOW)
+            lse_ref[head, rows, :] = highest + jnp.log(totals)
+        return carry
+
+    lax.fori_loop(0, heads, one_head, 0)
     put_chunks(part_refs, dot(mix_ref[...], out_full_ref[...]), width)
 
 
@@ -567,15 +578,13 @@
 
 
 def down_grad_body(*refs):
-    chunk_refs = refs[:-6]
-    square_ref, magnitude_ref, full_ref, left_ref, grad_ref, dact_ref = refs[-6:]
+    chunk_refs = refs[:-5]
+    square_ref, magnitude_ref, full_ref, grad_ref, dact_ref = refs[-5:]
     width = chunk_refs[0].shape[1]
-    tokens = grad_ref.shape[0]
     factor = magnitude_ref[...] / jnp.sqrt(square_ref[...])
     for k, ref in enumerate(chunk_refs):
         lanes = slice(k * width, (k + 1) * width)
-        grad_ref[:, lanes] = (ref[:tokens, :].astype(F32) * factor[:, lanes]).astype(LOW)
-        left_ref[:, lanes] = ref[tokens:, :]
+        grad_ref[:, lanes] = (ref[...].astype(F32) * factor[:, lanes]).astype(LOW)
     dact_ref[...] = dot(grad_ref[...], full_ref[...], 1, 1)
 
 
@@ -640,7 +649,7 @@
 
 
 def second_half_body(*refs):
-    count = (len(refs) - 16) // 2
+    count = (len(refs) - 18) // 2
     chunk_refs = refs[:count]
     (
         out_full_ref,
@@ -657,7 +666,8 @@
         full_ref,
     ) = refs[count : count + 12]
     all_ref, g_ref, scale_ref, token_ref = refs[count + 12 : count + 16]
-    part_refs = refs[count + 16 :]
+    part_refs = refs[count + 16 : -2]
+    mixed_ref, sum_ref = refs[-2:]
     tokens, width = chunk_refs[0].shape
     heads = width // HD
     for k, ref in enumerate(chunk_refs):
@@ -665,34 +675,45 @@
     mixed_grads = dot(all_ref[...], out_full_ref[...], 1, 1).astype(LOW)
     cosine = cos_ref[...]
     sine = sin_ref[...]
-    allowed = allowed_pairs(segr_ref[...], segc_ref[...])
-    token_total = jnp.zeros((tokens, HD), F32)
-    for head in range(heads):
-        at = head * HD
-        queries = q_ref[:, at : at + HD]
-        keys = k_ref[:, at : at + HD]
-        values = v_ref[:, at : at + HD]
-        mixed_grad = mixed_grads[:, at : at + HD]
-        logits = jnp.where(allowed, dot(queries, keys, 1, 1) * HD ** (-0.5), NEGATIVE)
-        probs = jnp.exp(logits - lse_ref[:, head : head + 1])
-        prob_grad = dot(mixed_grad, values, 1, 1)
-        delta = jnp.sum(prob_grad * probs, axis=1, keepdims=True)
-        raw_grad = (probs * (prob_grad - delta) * HD ** (-0.5)).astype(LOW)
-        query_grad = dot(raw_grad, keys)
-        key_grad = dot(raw_grad, queries, 0, 0)
-        value_grad = dot(probs.astype(LOW), mixed_grad, 0, 0)
+    mixed_ref[...] = mixed_grads
+    sum_ref[...] = jnp.zeros_like(sum_ref)
+
+    def one_head(head, carry):
+        at = pl.ds(pl.multiple_of(head * HD, HD), HD)
+        query_grads, key_grads, value_grads = [], [], []
+        for rows, seen in query_blocks(tokens):
+            mixed_grad = mixed_ref[rows, at]
+            logits = masked_logits(q_ref, k_ref, segr_ref, segc_ref, at, rows, seen)
+            probs = jnp.exp(logits - lse_ref[head, rows, :])
+            prob_grad = dot(mixed_grad, v_ref[seen, at], 1, 1)
+            delta = jnp.sum(prob_grad * probs, axis=1, keepdims=True)
+            raw_grad = (probs * (prob_grad - delta) * HD ** (-0.5)).astype(LOW)
+            query_grads.append(dot(raw_grad, k_ref[seen, at]))
+            key_grads.append(dot(raw_grad, q_ref[rows, at], 0, 0))
+            value_grads.append(dot(probs.astype(LOW), mixed_grad, 0, 0))
+
+        def joined(parts):
+            size = parts[0].shape[0]
+            return jnp.concatenate([parts[0] + parts[1][:size], parts[1][size:]], axis=0)
+
+        query_grad = jnp.concatenate(query_grads, axis=0)
+        key_grad = joined(key_grads)
         grads = (
             query_grad * cosine - halves_turned(query_grad) * sine,
             key_grad * cosine - halves_turned(key_grad) * sine,
-            value_grad,
+            joined(value_grads),
         )
         for member in range(3):
-            lanes = slice(member * width + at, member * width + at + HD)
+            lanes = pl.ds(pl.multiple_of(member * width + head * HD, HD), HD)
             shaped = proj_ref[:, lanes]
             lowered = (grads[member] * factor_ref[:, lanes]).astype(LOW)
             g_ref[:, lanes] = lowered
             scale_ref[:, lanes] = jnp.sum(grads[member] * shaped, axis=0, keepdims=True)
-            token_total = token_total + lowered.astype(F32) * shaped
+            sum_ref[...] += lowered.astype(F32) * shaped
+        return carry
+
+    lax.fori_loop(0, heads, one_head, 0)
+    token_total = sum_ref[...]
     token_ref[...] = lane_sums_as_row(token_total)
     for k, ref in enumerate(part_refs):
         ref[...] = dot(g_ref[...], full_ref[k * width : (k + 1) * width, :], 1, 1).astype(LOW)
@@ -751,7 +772,7 @@
     left_part, rights_out = column_adapters(
         low_ref[...],
         scaled_ref[...],
-        inner_product(scaled_ref[...], left_ref[...]),
+        dot(scaled_ref[...], left_ref[...], 1, 1),
         inverse_ref[...],
         full_ref[...],
         square_ref[...],
@@ -859,7 +880,6 @@
 
 def statistics_body(*refs):
     out_ref = refs[-1]
-    rows = lax.broadcasted_iota(jnp.int32, out_ref.shape, 0)
     lanes = lax.broadcasted_iota(jnp.int32, out_ref.shape, 1)
     table = jnp.zeros(out_ref.shape, F32)
     member = 0
@@ -872,7 +892,8 @@
             norm, drift = norms[:, taken], drifts[:, taken]
             first = jnp.sum(drift * drift, axis=1, keepdims=True)
             second = jnp.sum(norm, axis=1, keepdims=True)
-            table = jnp.where(rows == member, jnp.where(lanes == 0, first, second), table)
+            table = jnp.where(lanes == member, first, table)
+            table = jnp.where(lanes == member + 7, second, table)
             member += 1
     out_ref[...] = table
 
@@ -902,16 +923,15 @@
         own_factors(rights, magnitudes, width, hidden, hidden_padded, scalars)
     )
 
-    def lefts_of(members):
-        return split_rows(
-            SCALE * jnp.concatenate([lefts[member].T for member in members], axis=0)
-        )
+    def scaled_lefts(members):
+        return SCALE * jnp.concatenate([lefts[member].T for member in members], axis=0)
 
     own_one, *blocks_one = cut_blocks(weights[:3], width, width, scalars)
     extended = jnp.concatenate(
         [
             tokens,
-            lefts_of((0, 1, 2)),
+            split_rows(scaled_lefts((0, 1, 2))),
+            scaled_lefts((4, 5)).astype(LOW),
             attention_gain[None],
             feedforward_gain[None],
             jnp.zeros((14, width), LOW),
@@ -920,7 +940,7 @@
     )
     token_chunks = gather(extended)
     pieces_one = exchanged(blocks_one)
-    lefts_one, gain_two_all = gathered_lefts(token_chunks, token_count)
+    lefts_one, lefts_two, gain_two_all = gathered_lefts(token_chunks, token_count)
     weight_one, full_one, squares_one = assemble(
         own_one, pieces_one, lefts_one, rights_one, scalars, True
     )
@@ -942,21 +962,23 @@
     seg_rows = segments[:, None]
     seg_cols = segments[None, :]
 
-    left_out = lefts_of((3,))
-    left_down = pad_to(lefts_of((6,)), hidden_padded, 1)
+    left_out = split_rows(scaled_lefts((3,)))
+    left_down = pad_to(split_rows(scaled_lefts((6,))), hidden_padded, 1)
     full_out, high_out, squares_out, _, *cross_out = row_block(
         weights[3], left_out, rights[3], magnitudes[3][None], width, width, scalars
     )
     full_down, high_down, squares_down, magnitude_down_all, *cross_down = row_block(
         weights[6], left_down, rights[6], magnitudes[6][None], width, hidden_padded, scalars
     )
-    squares_all = total_relative(
+    squares_all, _ = total_relative(
         jnp.concatenate([squares_out, squares_down], axis=0)
         .reshape(2, count, width)
-        .transpose(1, 0, 2),
-    )
-    square_out, square_down = squares_all[0, :1], squares_all[0, 1:]
-    square_down_all = squares_all[:, 1].reshape(1, count * width)
+        .transpose(1, 0, 2)
+        .reshape(count, 2 * width),
+        jnp.zeros((0, 2 * width), F32),
+    )
+    square_out, square_down = squares_all[:1, :width], squares_all[:1, width:]
+    square_down_all = squares_all[:, width:].reshape(1, count * width)
     factor_out = magnitude_out / jnp.sqrt(square_out)
     factor_down = magnitude_down / jnp.sqrt(square_down)
 
@@ -981,7 +1003,7 @@
             ((token_count, 3 * R), F32),
         ]
         + [(chunk_shape, LOW)] * 4
-        + [((token_count, heads), F32), ((token_count, 1), F32), ((1, 3 * width), F32)]
+        + [((heads, token_count, 1), F32), ((token_count, 1), F32), ((1, 3 * width), F32)]
         + [(chunk_shape, LOW)] * count,
         *token_chunks,
         weight_one,
@@ -1006,14 +1028,10 @@
         factor_out,
     )
 
-    cotangent_chunks = gather(jnp.concatenate([cotangent, lefts_of((4, 5))], axis=0))
-    lefts_two, grad_down_all, grad_activated = kernel(
+    cotangent_chunks = gather(cotangent)
+    grad_down_all, grad_activated = kernel(
         down_grad_body,
-        [
-            ((4 * R, count * width), LOW),
-            ((token_count, count * width), LOW),
-            ((token_count, hidden_padded), F32),
-        ],
+        [((token_count, count * width), LOW), ((token_count, hidden_padded), F32)],
         *cotangent_chunks,
         square_down_all,
         magnitude_down_all,
@@ -1094,8 +1112,40 @@
         seg_rows,
         seg_cols,
         full_one,
-    )
-    token_one = total_over(token_one, "mp")
+        scratch=[pltpu.VMEM(chunk_shape, LOW), pltpu.VMEM((token_count, HD), F32)],
+    )
+    (stat_row,) = kernel(
+        statistics_body,
+        [((1, token_count), F32)],
+        squares_one,
+        magnitude_one,
+        square_out,
+        magnitude_out,
+        squares_two,
+        magnitude_two,
+        square_down,
+        magnitude_down,
+    )
+    own_ratios = jnp.concatenate(
+        [
+            negative_ratio(scale_out, magnitude_out, square_out),
+            negative_ratio(scale_down, magnitude_down, square_down),
+        ],
+        axis=1,
+    )
+    rows_wide = max(2 * width, token_count)
+    ratios_all, totals = total_relative(
+        pad_to(pad_to(own_ratios, count, 0), rows_wide, 1),
+        pad_to(jnp.concatenate([token_one, stat_row], axis=0), rows_wide, 1),
+    )
+    token_one = totals[:1, :token_count]
+    ratio_rows = jnp.concatenate(
+        [
+            ratios_all[:, slot * width : (slot + 1) * width].reshape(1, count * width)
+            for slot in range(2)
+        ],
+        axis=0,
+    )
     (input_gradient,) = kernel(
         input_grad_body,
         [(chunk_shape, F32)],
@@ -1122,15 +1172,6 @@
     )
     broad = total_over(broad, "dp")
 
-    ratio_rows = small_gather(
-        jnp.concatenate(
-            [
-                negative_ratio(scale_out, magnitude_out, square_out),
-                negative_ratio(scale_down, magnitude_down, square_down),
-            ],
-            axis=0,
-        ),
-    )
     slabs = hidden_padded // width
     rows_end, *bundles_end = kernel(
         end_adapters_body,
@@ -1189,19 +1230,7 @@
         squares_two[:, hidden_padded:],
         square_down,
     ]
-    (stat_sums,) = kernel(
-        statistics_body,
-        [((8, 128), F32)],
-        squares_one,
-        magnitude_one,
-        square_out,
-        magnitude_out,
-        squares_two,
-        magnitude_two,
-        square_down,
-        magnitude_down,
-    )
-    stat_sums = total_over(stat_sums, "mp")[:7, :2]
+    stat_sums = jnp.stack([totals[1, :7], totals[1, 7:14]], axis=1)
     columns_all = jnp.array([weight.shape[1] for weight in weights], F32)[:, None]
     means = stat_sums / columns_all
     statistics = jnp.concatenate([jnp.sqrt(means[:, :1]), means[:, 1:]], axis=1)

time: 501 us -> 532 us (1.062)
  the two profiles are of different devices: /device:TPU:0 before, /device:TPU:8 now
where the time goes in v2:
time: 532 us; the launch traced here: 522 us
  waiting for transfers between devices  215 us (40%)
  Pallas kernels  156 us (29%)
  starting transfers between devices  112 us (21%)
  other arithmetic  20.2 us (4%)
  local copies, waits for them, and re-layouts  17 us (3%)
    ppermute x93, waiting for transfers between devices, swap(): lax.ppermute(values, axis, [(place, place ^ offset) for place in range(co...  215 us
    pallas_call x31, Pallas kernels, kernel(): pl.pallas_call(body, out_shape=tuple((jax.ShapeDtypeStruct(shape, kind) f...  119 us
    ppermute x93, starting transfers between devices, swap(): lax.ppermute(values, axis, [(place, place ^ offset) for place in range(co...  112 us
    pallas_call x2, Pallas kernels, assemble(): pl.pallas_call(body if keep else body_alone, scratch_shapes=[] if keep el...  18.7 us
    pallas_call x2, Pallas kernels, by_rows(): pl.pallas_call(body, grid=(steps,), in_specs=[spec(operand.shape, slot <...  18.4 us
  transfers between devices with their start and end apart: 93, of which 35 were waited for; matrix products, arithmetic and copies ran while one was open for 4% of the time, Pallas kernels for 25%

profile of v2, /device:TPU:8, one launch (start us, length us, event | category | flops | bytes accessed | tf_op | source)
XLA Modules:
  0.0 521.9 jit_solution(1464332530125597447)
XLA Ops:
  4.0 4.3 shard_map.510
  8.3 6.7 %shard_map.515 = (bf16[768,2048]{1,0:T(8,128)(2,1)}, bf16[16,2048]{1,0:T(8,128)(2,1)}, f32[1,2048]{1,0:T(1,128)}, f32[1,2048]{1,0:T(1,128)}, bf16[4,16,256]{2,1,0:T(8,128)(2,1)}, /*index=5*/bf16[4,16,256]{2,1,0:T(8,128)(2,1)}) custom-call(s32[2]{0:T(128)} %pad_add_fusion.place_ref.refs_0_, bf16[704,2048]{1,0:T(8,128)(2,1)} %weight_ref.3, ...), custom_call_target="tpu_custom_call" | custom-call | tf_op jit(solution)/shard_map/pallas_call | solution.py:106
  26.7 5.2 %shard_map.517 = (bf16[256,1536]{1,0:T(8,128)(2,1)}, bf16[64,1536]{1,0:T(8,128)(2,1)}, bf16[64,1536]{1,0:T(8,128)(2,1)}, bf16[64,1536]{1,0:T(8,128)(2,1)}, bf16[...) custom-call(s32[2]{0:T(128)} %pad_add_fusion.place_ref.refs_0_, ...), custom_call_target="tpu_custom_call" | custom-call | tf_op jit(solution)/shard_map/pallas_call | solution.py:106
  44.3 27.4 %collective-permute-done.13.refs_6_ = bf16[64,768]{1,0:T(8,128)(2,1)S(1)} collective-permute-done((bf16[64,768]{1,0:T(8,128)(2,1)S(1)}, bf16[64,768]{1,0:T(8,128)(2,1)S(1)}, u32[]{:S(2)}, u32[]{:S(2)}) %collective-permute-start.13) | collective-permute-done | bytes 98336 | tf_op jit(solution)/shard_map/ppermute | solution.py:23
  80.6 20.1 %collective-permute-done.38.refs_4_ = bf16[64,1536]{1,0:T(8,128)(2,1)S(1)} collective-permute-done((bf16[64,1536]{1,0:T(8,128)(2,1)}, bf16[64,1536]{1,0:T(8,128)(2,1)S(1)}, u32[]{:S(2)}, u32[]{:S(2)}) %collective-permute-start.38) | collective-permute-done | bytes 196640 | tf_op jit(solution)/shard_map/ppermute | solution.py:23
  107.5 5.4 %collective-permute-start.1 = (bf16[656,256]{1,0:T(8,128)(2,1)S(1)}, bf16[656,256]{1,0:T(8,128)(2,1)}, u32[]{:S(2)}, u32[]{:S(2)}) collective-permute-start(bf16[656,256]{1,0:T(8,128)(2,1)S(1)} %concatenate.78.refs_0_), channel_id=1, source_target_pairs={{0,2},{1,3},{2,0},{3,1},{4,6},{5,7},{6,4},{7,5},{8,10},{9,11},{10,... | collective-permute-start | bytes 1007624 | tf_op jit(solution)/shard_map/ppermute | solution.py:23
  123.9 6.3 %collective-permute-done.6.refs_7_ = bf16[656,256]{1,0:T(8,128)(2,1)S(1)} collective-permute-done((bf16[656,256]{1,0:T(8,128)(2,1)S(1)}, bf16[656,256]{1,0:T(8,128)(2,1)S(1)}, u32[]{:S(2)}, u32[]{:S(2)}) %collective-permute-start.6) | collective-permute-done | bytes 335904 | tf_op jit(solution)/shard_map/ppermute | solution.py:23
  132.9 4.2 collective-permute-done.4.refs_5_
  153.0 8.4 %shard_map.509 = (bf16[2048,768]{1,0:T(8,128)(2,1)}, bf16[2048,768]{1,0:T(8,128)(2,1)}, f32[1,768]{1,0:T(1,128)}) custom-call(s32[2]{0:T(128)} %pad_add_fusion.place_ref.refs_0_, bf16[256,768]{1,0:T(8,128)(2,1)} %get-tuple-element.133.own_ref, bf16[96,2048]{1,0:T(8,128)(2,1)} %get-tuple-element.134.left_ref.refs_11_.refs_7_, ...), custom_call_target="tpu_custom_call" | custom-call | tf_op jit(solution)/shard_map/pallas_call | solution.py:331
  161.5 15.1 %shard_map.511 = (bf16[512,2048]{1,0:T(8,128)(2,1)}, f32[512,768]{1,0:T(8,128)}, f32[512,48]{1,0:T(8,128)}, bf16[512,256]{1,0:T(8,128)(2,1)}, bf16[512,256]{1,0:...) custom-call(bf16[656,256]{1,0:T(8,128)(2,1)} %copy-done.1, ...), custom_call_target="tpu_custom_call" | custom-call | tf_op jit(solution)/shard_map/pallas_call | solution.py:106
  180.4 5.7 %collective-permute-done.18.refs_1_ = bf16[512,256]{1,0:T(8,128)(2,1)S(1)} collective-permute-done((bf16[512,256]{1,0:T(8,128)(2,1)}, bf16[512,256]{1,0:T(8,128)(2,1)S(1)}, u32[]{:S(2)}, u32[]{:S(2)}) %collective-permute-start.18) | collective-permute-done | bytes 262176 | tf_op jit(solution)/shard_map/ppermute | solution.py:23
  187.0 4.7 collective-permute-done.20.refs_1_
  192.6 4.7 collective-permute-done.22.refs_1_
  207.0 7.2 %collective-permute-done.19.refs_2_ = bf16[512,256]{1,0:T(8,128)(2,1)S(1)} collective-permute-done((bf16[512,256]{1,0:T(8,128)(2,1)}, bf16[512,256]{1,0:T(8,128)(2,1)S(1)}, u32[]{:S(2)}, u32[]{:S(2)}) %collective-permute-start.19) | collective-permute-done | bytes 262176 | tf_op jit(solution)/shard_map/ppermute | solution.py:23
  215.4 8.1 %collective-permute-done.21.refs_3_ = bf16[512,256]{1,0:T(8,128)(2,1)S(1)} collective-permute-done((bf16[512,256]{1,0:T(8,128)(2,1)}, bf16[512,256]{1,0:T(8,128)(2,1)S(1)}, u32[]{:S(2)}, u32[]{:S(2)}) %collective-permute-start.21) | collective-permute-done | bytes 262176 | tf_op jit(solution)/shard_map/ppermute | solution.py:23
  225.0 4.8 collective-permute-done.23.refs_4_
  243.2 12.0 %collective-permute-done.32.refs_6_ = bf16[512,256]{1,0:T(8,128)(2,1)S(1)} collective-permute-done((bf16[512,256]{1,0:T(8,128)(2,1)}, bf16[512,256]{1,0:T(8,128)(2,1)S(1)}, u32[]{:S(2)}, u32[]{:S(2)}) %collective-permute-start.32) | collective-permute-done | bytes 262176 | tf_op jit(solution)/shard_map/ppermute | solution.py:23
  261.4 5.6 %shard_map.520 = (bf16[512,2048]{1,0:T(8,128)(2,1)}, f32[512,768]{1,0:T(8,128)}) custom-call(bf16[512,256]{1,0:T(8,128)(2,1)} %refs_5_.3, bf16[512,256]{1,0:T(8,128)(2,1)} %copy-done.16, bf16[512,256]{1,0:T(8,128)(2,1)} %copy-done.15, bf16[512,256]{1,0:T(8,128)(2,1)} %collective-permute-done.46.refs_3_, bf16[512,256]{1,0:T(8,128)(2,1)} %collective-permute-done.47.refs_4_, ...), custom_call_target="tpu_custom_call" | custom-call | tf_op jit(solution)/shard_map/pallas_call | solution.py:106
  267.1 10.3 %shard_map.519 = (bf16[2048,1536]{1,0:T(8,128)(2,1)}, f32[1,1536]{1,0:T(1,128)}) custom-call(s32[2]{0:T(128)} %pad_add_fusion.place_ref.refs_0_, bf16[256,1536]{1,0:T(8,128)(2,1)} %get-tuple-element.160.refs_1_, bf16[32,2048]{1,0:T(8,128)(2,1)} %get-tuple-element.161.refs_2_.left_ref, bf16[64,1536]{1,0:T(8,128)(2,1)} %get-tuple-element.162.refs_3_.right_ref, ...), custom_call_target="tpu_custom_call" | custom-call | tf_op jit(solution)/shard_map/pallas_call | solution.py:331
  278.3 13.5 %shard_map.521 = (bf16[512,2048]{1,0:T(8,128)(2,1)}, f32[512,1]{1,0:T(8,128)}, bf16[512,768]{1,0:T(8,128)(2,1)}, bf16[512,1536]{1,0:T(8,128)(2,1)}, f32[1,1536]{...) custom-call(bf16[512,256]{1,0:T(8,128)(2,1)} %get-tuple-element.158., ...), custom_call_target="tpu_custom_call" | custom-call | tf_op jit(solution)/shard_map/pallas_call | solution.py:124
  295.9 14.4 %collective-permute-done.65 = f32[1,512]{1,0:T(1,128)S(1)} collective-permute-done((f32[1,512]{1,0:T(1,128)}, f32[1,512]{1,0:T(1,128)S(1)}, u32[]{:S(2)}, u32[]{:S(2)}) %collective-permute-start.65) | collective-permute-done | bytes 2080 | tf_op jit(solution)/shard_map/ppermute | solution.py:23
  318.3 4.9 shard_map.522
  344.2 9.3 %shard_map.537 = (f32[40,768]{1,0:T(8,128)}, bf16[4,32,256]{2,1,0:T(8,128)(2,1)}, bf16[4,32,256]{2,1,0:T(8,128)(2,1)}) custom-call(bf16[512,1536]{1,0:T(8,128)(2,1)} %get-tuple-element.229.low_ref, bf16[512,2048]{1,0:T(8,128)(2,1)} %get-tuple-element.230.scaled_ref, f32[512,1]{1,0:T(8,128)} %get-tuple-element.196.refs_7_.inverse_ref, ...), custom_call_target="tpu_custom_call" | custom-call | tf_op jit(solution)/shard_map/pallas_call | solution.py:106
  369.5 19.2 %collective-permute-done.55.refs_3_ = bf16[512,256]{1,0:T(8,128)(2,1)S(1)} collective-permute-done((bf16[512,256]{1,0:T(8,128)(2,1)}, bf16[512,256]{1,0:T(8,128)(2,1)S(1)}, u32[]{:S(2)}, u32[]{:S(2)}) %collective-permute-start.55) | collective-permute-done | bytes 262176 | tf_op jit(solution)/shard_map/ppermute | solution.py:23
  389.6 6.3 %collective-permute-done.57.refs_4_ = bf16[512,256]{1,0:T(8,128)(2,1)S(1)} collective-permute-done((bf16[512,256]{1,0:T(8,128)(2,1)}, bf16[512,256]{1,0:T(8,128)(2,1)S(1)}, u32[]{:S(2)}, u32[]{:S(2)}) %collective-permute-start.57) | collective-permute-done | bytes 262176 | tf_op jit(solution)/shard_map/ppermute | solution.py:23
  410.7 5.6 %collective-permute-done.72.refs_5_ = bf16[512,256]{1,0:T(8,128)(2,1)S(1)} collective-permute-done((bf16[512,256]{1,0:T(8,128)(2,1)S(1)}, bf16[512,256]{1,0:T(8,128)(2,1)S(1)}, u32[]{:S(2)}, u32[]{:S(2)}) %collective-permute-start.72) | collective-permute-done | bytes 262176 | tf_op jit(solution)/shard_map/ppermute | solution.py:23
  416.3 4.9 collective-permute-done.70.refs_3_
  421.9 10.4 %shard_map.531 = (bf16[512,2048]{1,0:T(8,128)(2,1)}, bf16[512,768]{1,0:T(8,128)(2,1)}, f32[1,768]{1,0:T(1,128)}, f32[1,512]{1,0:T(1,128)}, bf16[512,256]{1,0:T(8...) custom-call(bf16[512,256]{1,0:T(8,128)(2,1)} %get-tuple-element.199., ...), custom_call_target="tpu_custom_call" | custom-call | tf_op jit(solution)/shard_map/pallas_call | solution.py:106
  444.6 11.5 %shard_map.538 = (f32[120,256]{1,0:T(8,128)}, bf16[4,144,256]{2,1,0:T(8,128)(2,1)}, bf16[4,144,256]{2,1,0:T(8,128)(2,1)}) custom-call(bf16[512,768]{1,0:T(8,128)(2,1)} %get-tuple-element.220.refs_0_, bf16[512,2048]{1,0:T(8,128)(2,1)} %get-tuple-element.221.refs_1_, f32[512,48]{1,0:T(8,128)} %get-tuple-element.222.refs_2_, ...), custom_call_target="tpu_custom_call" | custom-call | tf_op jit(solution)/shard_map/pallas_call | solution.py:106
  466.7 7.7 %collective-permute-done.85 = bf16[4,144,256]{2,1,0:T(8,128)(2,1)S(1)} collective-permute-done((bf16[4,144,256]{2,1,0:T(8,128)(2,1)}, bf16[4,144,256]{2,1,0:T(8,128)(2,1)S(1)}, u32[]{:S(2)}, u32[]{:S(2)}) %collective-permute-start.85) | collective-permute-done | bytes 294944 | tf_op jit(solution)/shard_map/ppermute | solution.py:23
  497.0 12.3 %collective-permute-done.79.refs_3_ = bf16[512,256]{1,0:T(8,128)(2,1)S(1)} collective-permute-done((bf16[512,256]{1,0:T(8,128)(2,1)}, bf16[512,256]{1,0:T(8,128)(2,1)S(1)}, u32[]{:S(2)}, u32[]{:S(2)}) %collective-permute-start.79) | collective-permute-done | bytes 262176 | tf_op jit(solution)/shard_map/ppermute | solution.py:23
  509.3 6.3 %collective-permute-done.81.refs_4_ = bf16[512,256]{1,0:T(8,128)(2,1)S(1)} collective-permute-done((bf16[512,256]{1,0:T(8,128)(2,1)}, bf16[512,256]{1,0:T(8,128)(2,1)S(1)}, u32[]{:S(2)}, u32[]{:S(2)}) %collective-permute-start.81) | collective-permute-done | bytes 262176 | tf_op jit(solution)/shard_map/ppermute | solution.py:23
  (485 shorter events, 227.3 us)
Async XLA Ops:
  34.0 40.5 %collective-permute-start.34 = (bf16[64,1536]{1,0:T(8,128)(2,1)}, bf16[64,1536]{1,0:T(8,128)(2,1)S(1)}, u32[]{:S(2)}, u32[]{:S(2)}) collective-permute-start(bf16[64,1536]{1,0:T(8,128)(2,1)} %get-tuple-element.163), channel_id=1, source_target_pairs={{0,1},{1,0},{2,3},{3,2},{4,5},{5,4},{6,7},{7,6},{8,9},{9,8},{10,11... | collective-permute-start | bytes 589832 | tf_op jit(solution)/shard_map/ppermute | solution.py:23
  35.6 39.1 %collective-permute-start.35 = (bf16[64,1536]{1,0:T(8,128)(2,1)}, bf16[64,1536]{1,0:T(8,128)(2,1)S(1)}, u32[]{:S(2)}, u32[]{:S(2)}) collective-permute-start(bf16[64,1536]{1,0:T(8,128)(2,1)} %get-tuple-element.164), channel_id=1, source_target_pairs={{0,2},{1,3},{2,0},{3,1},{4,6},{5,7},{6,4},{7,5},{8,10},{9,11},{10,... | collective-permute-start | bytes 589832 | tf_op jit(solution)/shard_map/ppermute | solution.py:23
  38.0 39.8 %collective-permute-start.36 = (bf16[64,1536]{1,0:T(8,128)(2,1)}, bf16[64,1536]{1,0:T(8,128)(2,1)S(1)}, u32[]{:S(2)}, u32[]{:S(2)}) collective-permute-start(bf16[64,1536]{1,0:T(8,128)(2,1)} %get-tuple-element.165), channel_id=1, source_target_pairs={{0,3},{1,2},{2,1},{3,0},{4,7},{5,6},{6,5},{7,4},{8,11},{9,10},{10,... | collective-permute-start | bytes 589832 | tf_op jit(solution)/shard_map/ppermute | solution.py:23
  39.5 39.6 %collective-permute-start.37 = (bf16[64,1536]{1,0:T(8,128)(2,1)}, bf16[64,1536]{1,0:T(8,128)(2,1)S(1)}, u32[]{:S(2)}, u32[]{:S(2)}) collective-permute-start(bf16[64,1536]{1,0:T(8,128)(2,1)} %get-tuple-element.166), channel_id=1, source_target_pairs={{0,4},{1,5},{2,6},{3,7},{4,0},{5,1},{6,2},{7,3},{8,12},{9,13},{10,... | collective-permute-start | bytes 589832 | tf_op jit(solution)/shard_map/ppermute | solution.py:23
  42.9 28.9 %collective-permute-start.13 = (bf16[64,768]{1,0:T(8,128)(2,1)S(1)}, bf16[64,768]{1,0:T(8,128)(2,1)S(1)}, u32[]{:S(2)}, u32[]{:S(2)}) collective-permute-start(bf16[64,768]{1,0:T(8,128)(2,1)S(1)} %copy-done.96), channel_id=1, source_target_pairs={{0,7},{1,6},{2,5},{3,4},{4,3},{5,2},{6,1},{7,0},{8,15},{9,14},{10,... | collective-permute-start | bytes 294920 | tf_op jit(solution)/shard_map/ppermute | solution.py:23
  71.8 44.8 %collective-permute-start.5 = (bf16[656,256]{1,0:T(8,128)(2,1)S(1)}, bf16[656,256]{1,0:T(8,128)(2,1)S(1)}, u32[]{:S(2)}, u32[]{:S(2)}) collective-permute-start(bf16[656,256]{1,0:T(8,128)(2,1)S(1)} %concatenate.78.refs_0_), channel_id=1, source_target_pairs={{0,6},{1,7},{2,4},{3,5},{4,2},{5,3},{6,0},{7,1},{8,14},{9,15},{10,... | collective-permute-start | bytes 1007624 | tf_op jit(solution)/shard_map/ppermute | solution.py:23
  74.5 43.6 %collective-permute-start.3 = (bf16[656,256]{1,0:T(8,128)(2,1)S(1)}, bf16[656,256]{1,0:T(8,128)(2,1)S(1)}, u32[]{:S(2)}, u32[]{:S(2)}) collective-permute-start(bf16[656,256]{1,0:T(8,128)(2,1)S(1)} %concatenate.78.refs_0_), channel_id=1, source_target_pairs={{0,4},{1,5},{2,6},{3,7},{4,0},{5,1},{6,2},{7,3},{8,12},{9,13},{10,... | collective-permute-start | bytes 1007624 | tf_op jit(solution)/shard_map/ppermute | solution.py:23
  74.6 26.0 %collective-permute-start.38 = (bf16[64,1536]{1,0:T(8,128)(2,1)}, bf16[64,1536]{1,0:T(8,128)(2,1)S(1)}, u32[]{:S(2)}, u32[]{:S(2)}) collective-permute-start(bf16[64,1536]{1,0:T(8,128)(2,1)} %get-tuple-element.167), channel_id=1, source_target_pairs={{0,5},{1,4},{2,7},{3,6},{4,1},{5,0},{6,3},{7,2},{8,13},{9,12},{10,... | collective-permute-start | bytes 589832 | tf_op jit(solution)/shard_map/ppermute | solution.py:23
  77.9 26.4 %collective-permute-start.39 = (bf16[64,1536]{1,0:T(8,128)(2,1)}, bf16[64,1536]{1,0:T(8,128)(2,1)S(1)}, u32[]{:S(2)}, u32[]{:S(2)}) collective-permute-start(bf16[64,1536]{1,0:T(8,128)(2,1)} %get-tuple-element.168), channel_id=1, source_target_pairs={{0,6},{1,7},{2,4},{3,5},{4,2},{5,3},{6,0},{7,1},{8,14},{9,15},{10,... | collective-permute-start | bytes 589832 | tf_op jit(solution)/shard_map/ppermute | solution.py:23
  79.1 52.0 %collective-permute-start.15 = (bf16[7,64,768]{2,1,0:T(8,128)(2,1)}, bf16[7,64,768]{2,1,0:T(8,128)(2,1)}, u32[]{:S(2)}, u32[]{:S(2)}) collective-permute-start(bf16[7,64,768]{2,1,0:T(8,128)(2,1)} %shard_map.508.refs_0_), channel_id=1, source_target_pairs={{0,16},{8,24},{16,0},{24,8},{1,17},{9,25},{17,1},{25,9},{2,18},{10... | collective-permute-start | bytes 2064392 | tf_op jit(solution)/shard_map/ppermute | solution.py:23
  116.5 63.1 %collective-permute-start.42 = (bf16[7,64,1536]{2,1,0:T(8,128)(2,1)}, bf16[7,64,1536]{2,1,0:T(8,128)(2,1)S(1)}, u32[]{:S(2)}, u32[]{:S(2)}) collective-permute-start(bf16[7,64,1536]{2,1,0:T(8,128)(2,1)} %shard_map.518.refs_4_), channel_id=1, source_target_pairs={{0,16},{8,24},{16,0},{24,8},{1,17},{9,25},{17,1},{25,9},{2,18},{10... | collective-permute-start | bytes 4128776 | tf_op jit(solution)/shard_map/ppermute | solution.py:23
  137.2 41.6 %collective-permute-start.49 = (bf16[512,256]{1,0:T(8,128)(2,1)S(1)}, bf16[512,256]{1,0:T(8,128)(2,1)}, u32[]{:S(2)}, u32[]{:S(2)}) collective-permute-start(bf16[512,256]{1,0:T(8,128)(2,1)S(1)} %copy-done.4), channel_id=1, source_target_pairs={{0,6},{1,7},{2,4},{3,5},{4,2},{5,3},{6,0},{7,1},{8,14},{9,15},{10,... | collective-permute-start | bytes 786440 | tf_op jit(solution)/shard_map/ppermute | solution.py:23
  140.8 38.9 %collective-permute-start.47 = (bf16[512,256]{1,0:T(8,128)(2,1)S(1)}, bf16[512,256]{1,0:T(8,128)(2,1)}, u32[]{:S(2)}, u32[]{:S(2)}) collective-permute-start(bf16[512,256]{1,0:T(8,128)(2,1)S(1)} %copy-done.4), channel_id=1, source_target_pairs={{0,4},{1,5},{2,6},{3,7},{4,0},{5,1},{6,2},{7,3},{8,12},{9,13},{10,... | collective-permute-start | bytes 786440 | tf_op jit(solution)/shard_map/ppermute | solution.py:23
  141.2 36.4 %collective-permute-start.26 = (f32[8,512]{1,0:T(8,128)S(1)}, f32[8,512]{1,0:T(8,128)S(1)}, u32[]{:S(2)}, u32[]{:S(2)}) collective-permute-start(f32[8,512]{1,0:T(8,128)S(1)} %pad_maximum_fusion.8), channel_id=1, source_target_pairs={{0,4},{1,5},{2,6},{3,7},{4,0},{5,1},{6,2},{7,3},{8,12},{9,13},{10,... | collective-permute-start | bytes 49160 | tf_op jit(solution)/shard_map/ppermute | solution.py:23
  179.7 62.4 %collective-permute-start.41 = (bf16[7,64,1536]{2,1,0:T(8,128)(2,1)S(1)}, bf16[7,64,1536]{2,1,0:T(8,128)(2,1)}, u32[]{:S(2)}, u32[]{:S(2)}) collective-permute-start(bf16[7,64,1536]{2,1,0:T(8,128)(2,1)S(1)} %copy-done), channel_id=1, source_target_pairs={{0,8},{8,0},{16,24},{24,16},{1,9},{9,1},{17,25},{25,17},{2,10},{10... | collective-permute-start | bytes 4128776 | tf_op jit(solution)/shard_map/ppermute | solution.py:23
  197.3 69.7 %collective-permute-start.43 = (bf16[7,64,1536]{2,1,0:T(8,128)(2,1)S(1)}, bf16[7,64,1536]{2,1,0:T(8,128)(2,1)}, u32[]{:S(2)}, u32[]{:S(2)}) collective-permute-start(bf16[7,64,1536]{2,1,0:T(8,128)(2,1)S(1)} %collective-permute-done.42.refs_6_), channel_id=1, source_target_pairs={{0,8},{8,0},{16,24},{24,16},{1,9},{9,1},{17,25},{25,17},{2,10},{10... | collective-permute-start | bytes 4128776 | tf_op jit(solution)/shard_map/ppermute | solution.py:23
  242.1 35.3 %collective-permute-start.27 = (bf16[512,256]{1,0:T(8,128)(2,1)}, bf16[512,256]{1,0:T(8,128)(2,1)S(1)}, u32[]{:S(2)}, u32[]{:S(2)}) collective-permute-start(bf16[512,256]{1,0:T(8,128)(2,1)} %get-tuple-element.158.refs_0_), channel_id=1, source_target_pairs={{0,1},{1,0},{2,3},{3,2},{4,5},{5,4},{6,7},{7,6},{8,9},{9,8},{10,11... | collective-permute-start | bytes 786440 | tf_op jit(solution)/shard_map/ppermute | solution.py:23
  291.8 33.2 %collective-permute-start.59 = (bf16[512,256]{1,0:T(8,128)(2,1)}, bf16[512,256]{1,0:T(8,128)(2,1)S(1)}, u32[]{:S(2)}, u32[]{:S(2)}) collective-permute-start(bf16[512,256]{1,0:T(8,128)(2,1)} %get-tuple-element.191), channel_id=1, source_target_pairs={{0,1},{1,0},{2,3},{3,2},{4,5},{5,4},{6,7},{7,6},{8,9},{9,8},{10,11... | collective-permute-start | bytes 786440 | tf_op jit(solution)/shard_map/ppermute | solution.py:23
  292.4 32.9 %collective-permute-start.61 = (bf16[512,256]{1,0:T(8,128)(2,1)}, bf16[512,256]{1,0:T(8,128)(2,1)S(1)}, u32[]{:S(2)}, u32[]{:S(2)}) collective-permute-start(bf16[512,256]{1,0:T(8,128)(2,1)} %get-tuple-element.193), channel_id=1, source_target_pairs={{0,1},{1,0},{2,3},{3,2},{4,5},{5,4},{6,7},{7,6},{8,9},{9,8},{10,11... | collective-permute-start | bytes 786440 | tf_op jit(solution)/shard_map/ppermute | solution.py:23
  293.9 34.9 %collective-permute-start.63 = (bf16[512,256]{1,0:T(8,128)(2,1)}, bf16[512,256]{1,0:T(8,128)(2,1)S(1)}, u32[]{:S(2)}, u32[]{:S(2)}) collective-permute-start(bf16[512,256]{1,0:T(8,128)(2,1)} %get-tuple-element.195), channel_id=1, source_target_pairs={{0,1},{1,0},{2,3},{3,2},{4,5},{5,4},{6,7},{7,6},{8,9},{9,8},{10,11... | collective-permute-start | bytes 786440 | tf_op jit(solution)/shard_map/ppermute | solution.py:23
  328.9 24.6 %collective-permute-start.60 = (bf16[512,256]{1,0:T(8,128)(2,1)}, bf16[512,256]{1,0:T(8,128)(2,1)S(1)}, u32[]{:S(2)}, u32[]{:S(2)}) collective-permute-start(bf16[512,256]{1,0:T(8,128)(2,1)} %shard_map.527), channel_id=1, source_target_pairs={{0,2},{1,3},{2,0},{3,1},{4,6},{5,7},{6,4},{7,5},{8,10},{9,11},{10,... | collective-permute-start | bytes 786440 | tf_op jit(solution)/shard_map/ppermute | solution.py:23
  332.6 25.3 %collective-permute-start.62 = (bf16[512,256]{1,0:T(8,128)(2,1)}, bf16[512,256]{1,0:T(8,128)(2,1)S(1)}, u32[]{:S(2)}, u32[]{:S(2)}) collective-permute-start(bf16[512,256]{1,0:T(8,128)(2,1)} %shard_map.528), channel_id=1, source_target_pairs={{0,4},{1,5},{2,6},{3,7},{4,0},{5,1},{6,2},{7,3},{8,12},{9,13},{10,... | collective-permute-start | bytes 786440 | tf_op jit(solution)/shard_map/ppermute | solution.py:23
  334.7 25.4 %collective-permute-start.64 = (bf16[512,256]{1,0:T(8,128)(2,1)}, bf16[512,256]{1,0:T(8,128)(2,1)S(1)}, u32[]{:S(2)}, u32[]{:S(2)}) collective-permute-start(bf16[512,256]{1,0:T(8,128)(2,1)} %shard_map.529), channel_id=1, source_target_pairs={{0,6},{1,7},{2,4},{3,5},{4,2},{5,3},{6,0},{7,1},{8,14},{9,15},{10,... | collective-permute-start | bytes 786440 | tf_op jit(solution)/shard_map/ppermute | solution.py:23
  338.3 27.1 %collective-permute-start.51 = (bf16[512,256]{1,0:T(8,128)(2,1)S(1)}, bf16[512,256]{1,0:T(8,128)(2,1)S(1)}, u32[]{:S(2)}, u32[]{:S(2)}) collective-permute-start(bf16[512,256]{1,0:T(8,128)(2,1)S(1)} %copy-done.95), channel_id=1, source_target_pairs={{0,1},{1,0},{2,3},{3,2},{4,5},{5,4},{6,7},{7,6},{8,9},{9,8},{10,11... | collective-permute-start | bytes 786440 | tf_op jit(solution)/shard_map/ppermute | solution.py:23
  357.8 30.8 %collective-permute-start.55 = (bf16[512,256]{1,0:T(8,128)(2,1)}, bf16[512,256]{1,0:T(8,128)(2,1)S(1)}, u32[]{:S(2)}, u32[]{:S(2)}) collective-permute-start(bf16[512,256]{1,0:T(8,128)(2,1)} %shard_map.524), channel_id=1, source_target_pairs={{0,4},{1,5},{2,6},{3,7},{4,0},{5,1},{6,2},{7,3},{8,12},{9,13},{10,... | collective-permute-start | bytes 786440 | tf_op jit(solution)/shard_map/ppermute | solution.py:23
  360.2 35.7 %collective-permute-start.57 = (bf16[512,256]{1,0:T(8,128)(2,1)}, bf16[512,256]{1,0:T(8,128)(2,1)S(1)}, u32[]{:S(2)}, u32[]{:S(2)}) collective-permute-start(bf16[512,256]{1,0:T(8,128)(2,1)} %shard_map.525), channel_id=1, source_target_pairs={{0,6},{1,7},{2,4},{3,5},{4,2},{5,3},{6,0},{7,1},{8,14},{9,15},{10,... | collective-permute-start | bytes 786440 | tf_op jit(solution)/shard_map/ppermute | solution.py:23
  364.3 37.2 %collective-permute-start.73 = (bf16[512,256]{1,0:T(8,128)(2,1)}, bf16[512,256]{1,0:T(8,128)(2,1)S(1)}, u32[]{:S(2)}, u32[]{:S(2)}) collective-permute-start(bf16[512,256]{1,0:T(8,128)(2,1)} %get-tuple-element.199.refs_0_), channel_id=1, source_target_pairs={{0,6},{1,7},{2,4},{3,5},{4,2},{5,3},{6,0},{7,1},{8,14},{9,15},{10,... | collective-permute-start | bytes 786440 | tf_op jit(solution)/shard_map/ppermute | solution.py:23
  365.4 40.1 %collective-permute-start.71 = (bf16[512,256]{1,0:T(8,128)(2,1)}, bf16[512,256]{1,0:T(8,128)(2,1)S(1)}, u32[]{:S(2)}, u32[]{:S(2)}) collective-permute-start(bf16[512,256]{1,0:T(8,128)(2,1)} %get-tuple-element.199.refs_0_), channel_id=1, source_target_pairs={{0,4},{1,5},{2,6},{3,7},{4,0},{5,1},{6,2},{7,3},{8,12},{9,13},{10,... | collective-permute-start | bytes 786440 | tf_op jit(solution)/shard_map/ppermute | solution.py:23
  367.9 38.9 %collective-permute-start.69 = (bf16[512,256]{1,0:T(8,128)(2,1)}, bf16[512,256]{1,0:T(8,128)(2,1)S(1)}, u32[]{:S(2)}, u32[]{:S(2)}) collective-permute-start(bf16[512,256]{1,0:T(8,128)(2,1)} %get-tuple-element.199.refs_0_), channel_id=1, source_target_pairs={{0,2},{1,3},{2,0},{3,1},{4,6},{5,7},{6,4},{7,5},{8,10},{9,11},{10,... | collective-permute-start | bytes 786440 | tf_op jit(solution)/shard_map/ppermute | solution.py:23
  388.7 45.8 %collective-permute-start.92 = (f32[40,768]{1,0:T(8,128)S(1)}, f32[40,768]{1,0:T(8,128)S(1)}, u32[]{:S(2)}, u32[]{:S(2)}) collective-permute-start(f32[40,768]{1,0:T(8,128)S(1)} %add.94), channel_id=1, source_target_pairs={{0,16},{8,24},{16,0},{24,8},{1,17},{9,25},{17,1},{25,9},{2,18},{10... | collective-permute-start | bytes 368648 | tf_op jit(solution)/shard_map/ppermute | solution.py:23
  457.7 38.2 %collective-permute-start.75 = (bf16[512,256]{1,0:T(8,128)(2,1)S(1)}, bf16[512,256]{1,0:T(8,128)(2,1)S(1)}, u32[]{:S(2)}, u32[]{:S(2)}) collective-permute-start(bf16[512,256]{1,0:T(8,128)(2,1)S(1)} %copy-done.91), channel_id=1, source_target_pairs={{0,1},{1,0},{2,3},{3,2},{4,5},{5,4},{6,7},{7,6},{8,9},{9,8},{10,11... | collective-permute-start | bytes 786440 | tf_op jit(solution)/shard_map/ppermute | solution.py:23
  494.3 24.7 %collective-permute-start.90 = (f32[232,256]{1,0:T(8,128)S(1)}, f32[232,256]{1,0:T(8,128)S(1)}, u32[]{:S(2)}, u32[]{:S(2)}) collective-permute-start(f32[232,256]{1,0:T(8,128)S(1)} %add.91), channel_id=1, source_target_pairs={{0,16},{8,24},{16,0},{24,8},{1,17},{9,25},{17,1},{25,9},{2,18},{10... | collective-permute-start | bytes 712712 | tf_op jit(solution)/shard_map/ppermute | solution.py:23
  (163 other events, 2623.2 us)
